TPU v7x, 256 devices: a whole 4x4x8 slice. The times are simulated.
256 devices in a mesh: nbhd: 16 (over y_lo, x, core), sub: 16 (over z, y_hi).
Axes of the slice: x: 4, y: 4 (y_hi: 2, y_lo: 2; y = y_hi * 2 + y_lo), z: 8, core: 2. Of those that a mesh axis runs over, the one named last changes fastest.
Arguments:
- snap_init: bfloat16 [16, 64, 16, 96, 128], P('nbhd', 'sub'), may hold values from -8 to 8
- channel_map: int32 [16, 64, 16, 96], P('nbhd', 'sub'), may hold values from 0 to 3
- yface_vals: bfloat16 [16, 96, 128], P('nbhd'), may hold values from -6 to 6
- zface_vals: bfloat16 [16, 16, 128], P('nbhd'), may hold values from -6 to 6
- face_of: int32 [16, 128], P('nbhd'), may hold values from 0 to 3
- start_block: float32 [16, 128, 32], P('nbhd'), may hold values from -6 to 6
- correlation: int32 [16, 16], replicated, may hold values 0 or 1
Outputs:
- owner_basis: bfloat16 [16, 16, 16, 32, 384], P('nbhd', 'sub')
All inputs are finite; a program needn't handle non-finite values.
Results may differ from a plain program's by a relative error of at most 0.0072.
Values may be sent and summed in bfloat16 or wider, within the bound.
A program may use at most 128 MiB of HBM per device.

v0:
```python
import jax
import jax.numpy as jnp
from jax import lax
from jax.sharding import PartitionSpec as P

SWEEPS = 3
ITERS = 4


def with_halo(cells, sides, width):
    for axis, dim in sides:
        count = lax.axis_size(axis)
        ends = count - 1
        head = lax.slice_in_dim(cells, 0, width, axis=dim)
        tail = lax.slice_in_dim(cells, cells.shape[dim] - width, cells.shape[dim], axis=dim)
        cells = jnp.concatenate(
            [
                lax.ppermute(tail, axis, [(i, (i + 1) % count) for i in range(ends)]),
                cells,
                lax.ppermute(head, axis, [((i + 1) % count, i) for i in range(ends)]),
            ],
            axis=dim,
        )
    return cells


def harmonic(left_k, right_k):
    return 2.0 * left_k * right_k / (left_k + right_k)


def face_terms(field_ext, kappa_ext, first_plane, plane_count, ghosts):
    length = field_ext.shape[0]
    plane_ids = first_plane + jnp.arange(length, dtype=jnp.int32)
    inside = (plane_ids >= 0) & (plane_ids < plane_count)
    kappa = jnp.where(inside[:, None, None], kappa_ext, jnp.float32(1.0))
    centre = kappa[1:-1]
    x_lower = jnp.where(inside[:-2, None, None], harmonic(centre, kappa[:-2]), centre)
    x_upper = jnp.where(inside[2:, None, None], harmonic(centre, kappa[2:]), centre)
    y_inner = harmonic(centre[:, 1:], centre[:, :-1])
    y_lower = jnp.concatenate([centre[:, :1], y_inner], axis=1)
    y_upper = jnp.concatenate([y_inner, centre[:, -1:]], axis=1)
    z_inner = harmonic(centre[:, :, 1:], centre[:, :, :-1])
    z_lower = jnp.concatenate([centre[:, :, :1], z_inner], axis=2)
    z_upper = jnp.concatenate([z_inner, centre[:, :, -1:]], axis=2)
    middle = field_ext[1:-1].astype(jnp.float32)
    count, rows_y, rows_z, width = middle.shape
    ghost_ylo, ghost_yhi, ghost_zlo, ghost_zhi = ghosts
    below_y = jnp.concatenate(
        [jnp.broadcast_to(ghost_ylo, (count, 1, rows_z, width)), middle[:, :-1]], axis=1
    )
    above_y = jnp.concatenate(
        [middle[:, 1:], jnp.broadcast_to(ghost_yhi, (count, 1, rows_z, width))], axis=1
    )
    below_z = jnp.concatenate(
        [jnp.broadcast_to(ghost_zlo[:, None, :], (count, rows_y, 1, width)), middle[:, :, :-1]],
        axis=2,
    )
    above_z = jnp.concatenate(
        [middle[:, :, 1:], jnp.broadcast_to(ghost_zhi[:, None, :], (count, rows_y, 1, width))],
        axis=2,
    )
    numer = (
        x_lower[..., None] * field_ext[:-2].astype(jnp.float32)
        + x_upper[..., None] * field_ext[2:].astype(jnp.float32)
        + y_lower[..., None] * below_y
        + y_upper[..., None] * above_y
        + z_lower[..., None] * below_z
        + z_upper[..., None] * above_z
    )
    denom = x_lower + x_upper + y_lower + y_upper + z_lower + z_upper
    return (numer, denom, middle, inside[1:-1])


def relax(field_ext, kappa_ext, first_plane, plane_count, ghosts):
    numer, denom, middle, inside = face_terms(
        field_ext, kappa_ext, first_plane, plane_count, ghosts
    )
    updated = numer / denom[..., None]
    return jnp.where(inside[:, None, None, None], updated, jnp.float32(0.0)).astype(jnp.bfloat16)


def stiffness(field_ext, kappa_ext, first_plane, plane_count):
    rows_y, rows_z, width = (field_ext.shape[1], field_ext.shape[2], field_ext.shape[3])
    zero_y = jnp.zeros((rows_z, width), jnp.float32)
    zero_z = jnp.zeros((rows_y, width), jnp.float32)
    numer, denom, middle, inside = face_terms(
        field_ext, kappa_ext, first_plane, plane_count, (zero_y, zero_y, zero_z, zero_z)
    )
    return (denom[..., None] * middle - numer).astype(jnp.bfloat16)


def make_ghosts(y_values, z_values, face_ids):
    y_float = y_values.astype(jnp.float32)
    z_float = z_values.astype(jnp.float32)
    picks = [(face_ids == side).astype(jnp.float32)[None, :] for side in range(4)]
    return (y_float * picks[0], y_float * picks[1], z_float * picks[2], z_float * picks[3])


def gram_terms(snapshots, kappa, stiff_apply):
    width = snapshots.shape[-1]
    flat = snapshots.reshape(-1, width)
    weighted = (flat * (kappa.reshape(-1, 1) / 16.0)).astype(jnp.bfloat16)
    stiff_flat = stiff_apply.reshape(-1, width)
    dims = (((0,), (0,)), ((), ()))
    mass_part = lax.dot_general(flat, weighted, dims, preferred_element_type=jnp.float32)
    stiff_part = lax.dot_general(flat, stiff_flat, dims, preferred_element_type=jnp.float32)
    return (mass_part, stiff_part)


def subspace(mass_sum, stiff_sum, start, cell_count):
    highest = lax.Precision.HIGHEST
    mass_gram = mass_sum / cell_count
    stiff_gram = (stiff_sum + stiff_sum.T) * (0.5 / cell_count)
    factor = jnp.linalg.cholesky(stiff_gram)
    mode_block = start
    for step in range(ITERS):
        right_side = jnp.dot(mass_gram, mode_block, precision=highest)
        solved = jax.scipy.linalg.cho_solve((factor, True), right_side)
        inner = jnp.dot(solved.T, jnp.dot(mass_gram, solved, precision=highest), precision=highest)
        inner = 0.5 * (inner + inner.T)
        lower = jnp.linalg.cholesky(inner)
        mode_block = jax.scipy.linalg.solve_triangular(lower, solved.T, lower=True).T
    return mode_block


def on_device(snap_init, channel_map, yface_vals, zface_vals, face_of, start_block, correlation):
    initial = snap_init[0]
    class_map = channel_map[0]
    planes = initial.shape[0]
    plane_count = planes * lax.axis_size("sub")
    base_plane = lax.axis_index("sub") * planes
    ghosts = make_ghosts(yface_vals[0], zface_vals[0], face_of[0])
    class_ext = with_halo(class_map, (("sub", 0),), 1)
    kappa_edge = jnp.exp2(2.0 * class_ext.astype(jnp.float32))
    state = initial
    for sweep_no in range(SWEEPS):
        padded = with_halo(state, (("sub", 0),), 1)
        state = relax(padded, kappa_edge, base_plane - 1, plane_count, ghosts)
    field_edge = with_halo(state, (("sub", 0),), 1)
    snapshots = field_edge[1:-1]
    kappa_local = kappa_edge[1:-1]
    stiff_apply = stiffness(field_edge, kappa_edge, base_plane - 1, plane_count)
    mass_part, stiff_part = gram_terms(snapshots, kappa_local, stiff_apply)
    mass_sum, stiff_sum = lax.psum((mass_part, stiff_part), "sub")
    cell_count = float(plane_count * snapshots.shape[1] * snapshots.shape[2])
    mode_block = subspace(mass_sum, stiff_sum, start_block[0], cell_count)
    owner_count = lax.axis_size("nbhd")
    width = snapshots.shape[-1]
    piece_cells = snapshots.size // width // owner_count
    blocks = snapshots.reshape(owner_count, piece_cells, width)
    pieces = jnp.einsum(
        "pcs,sm->pmc", blocks, mode_block.astype(jnp.bfloat16), preferred_element_type=jnp.float32
    ).astype(jnp.bfloat16)
    received = lax.all_to_all(pieces, "nbhd", split_axis=0, concat_axis=0, tiled=True)
    column = lax.dynamic_slice_in_dim(correlation, lax.axis_index("nbhd"), 1, axis=1)[:, 0]
    result = received * column.astype(jnp.bfloat16)[:, None, None]
    return result[None, None]


def solution(mesh):
    return jax.shard_map(
        on_device,
        mesh=mesh,
        in_specs=(
            P("nbhd", "sub", None, None, None),
            P("nbhd", "sub", None, None),
            P("nbhd", None, None),
            P("nbhd", None, None),
            P("nbhd", None),
            P("nbhd", None, None),
            P(),
        ),
        out_specs=P("nbhd", "sub", None, None, None),
        check_vma=False,
    )
```

profile of v0, /device:TPU:1, one launch (start us, length us, event | category | flops | bytes accessed | tf_op | source)
XLA Modules:
  0.0 397.7 jit_solution(11359488250215993704)
XLA Ops:
  7.9 6.2 %collective-permute-start = (s32[1,16,96]{2,1,0:T(8,128)}, s32[1,16,96]{2,1,0:T(8,128)}, u32[]{:S(2)}, u32[]{:S(2)}) collective-permute-start(s32[1,16,96]{2,1,0:T(8,128)} %get-tuple-element.47), channel_id=1, source_target_pairs={{0,1},{1,2},{2,3},{3,4},{4,5},{5,6},{6,7},{7,8},{8,9},{9,10},{10,1... | collective-permute-start | bytes 18440 | tf_op jit(solution)/shard_map/ppermute | solution.py:18
  17.3 6.2 %collective-permute-start.2 = (bf16[1,16,96,128]{3,2,1,0:T(8,128)(2,1)}, bf16[1,16,96,128]{3,2,1,0:T(8,128)(2,1)}, u32[]{:S(2)}, u32[]{:S(2)}) collective-permute-start(bf16[1,16,96,128]{3,2,1,0:T(8,128)(2,1)} %get-tuple-element.39), channel_id=1, source_target_pairs={{0,1},{1,2},{2,3},{3,4},{4,5},{5,6},{6,7},{7,8},{8,9},{9,10},{10,1... | collective-permute-start | bytes 1179656 | tf_op jit(solution)/shard_map/ppermute | solution.py:18
  26.6 3.3 fusion.140
  29.9 2.4 fusion.141
  35.6 3.0 collective-permute-done.2
  38.8 9.9 %fusion.32 = bf16[4,16,96,128]{3,2,1,0:T(8,128)(2,1)S(1)} fusion(f32[4,16,1,128]{3,2,1,0:T(1,128)S(1)} %broadcast_in_dim.163, f32[4,16,95,128]{3,2,1,0:T(8,128)} %get-tuple-element.20, f32[4,16,95,128]{3,2,1,0:T(8,128)S(1)} %get-tuple-element.19, f32[4,16,1,128]{3,2,1,0:T(1,128)S(1)} %broadcast_in_dim.162, f32[4,1,96,128]{3,2,1,0:T(8,128)S(1)} %broadcast_in_dim.161, ...), kind=kLoop, calls=%fused_computation.46 | loop fusion | flops 17301504 | bytes 16687108 | tf_op jit(solution)/shard_map/convert_element_type | solution.py:79
  49.9 5.6 %collective-permute-start.4 = (bf16[1,16,96,128]{3,2,1,0:T(8,128)(2,1)S(1)}, bf16[1,16,96,128]{3,2,1,0:T(8,128)(2,1)S(1)}, u32[]{:S(2)}, u32[]{:S(2)}) collective-permute-start(bf16[1,16,96,128]{3,2,1,0:T(8,128)(2,1)S(1)} %get-tuple-element.33), channel_id=1, source_target_pairs={{0,1},{1,2},{2,3},{3,4},{4,5},{5,6},{6,7},{7,8},{8,9},{9,10},{10,1... | collective-permute-start | bytes 1179656 | tf_op jit(solution)/shard_map/ppermute | solution.py:18
  57.6 4.2 %collective-permute-done.4 = bf16[1,16,96,128]{3,2,1,0:T(8,128)(2,1)S(1)} collective-permute-done((bf16[1,16,96,128]{3,2,1,0:T(8,128)(2,1)S(1)}, bf16[1,16,96,128]{3,2,1,0:T(8,128)(2,1)S(1)}, u32[]{:S(2)}, u32[]{:S(2)}) %collective-permute-start.4) | collective-permute-done | bytes 393248 | tf_op jit(solution)/shard_map/ppermute | solution.py:18
  61.8 8.0 %collective-permute-done.5 = bf16[1,16,96,128]{3,2,1,0:T(8,128)(2,1)S(1)} collective-permute-done((bf16[1,16,96,128]{3,2,1,0:T(8,128)(2,1)S(1)}, bf16[1,16,96,128]{3,2,1,0:T(8,128)(2,1)S(1)}, u32[]{:S(2)}, u32[]{:S(2)}) %collective-permute-start.5) | collective-permute-done | bytes 393248 | tf_op jit(solution)/shard_map/ppermute | solution.py:20
  69.8 6.8 %fusion.31 = bf16[4,16,96,128]{3,2,1,0:T(8,128)(2,1)S(1)} fusion(f32[4,16,1,128]{3,2,1,0:T(1,128)S(1)} %broadcast_in_dim.163, f32[4,16,95,128]{3,2,1,0:T(8,128)S(1)} %get-tuple-element.38, f32[4,16,95,128]{3,2,1,0:T(8,128)S(1)} %get-tuple-element.37, f32[4,16,1,128]{3,2,1,0:T(1,128)S(1)} %broadcast_in_dim.162, f32[4,1,96,128]{3,2,1,0:T(8,128)S(1)} %broadcast_in_dim.161, ...), kind=kLoop, calls=%fused_computation.45 | loop fusion | flops 17301504 | bytes 16687108 | tf_op jit(solution)/shard_map/convert_element_type | solution.py:79
  77.9 6.3 %collective-permute-start.6 = (bf16[1,16,96,128]{3,2,1,0:T(8,128)(2,1)S(1)}, bf16[1,16,96,128]{3,2,1,0:T(8,128)(2,1)S(1)}, u32[]{:S(2)}, u32[]{:S(2)}) collective-permute-start(bf16[1,16,96,128]{3,2,1,0:T(8,128)(2,1)S(1)} %get-tuple-element.27), channel_id=1, source_target_pairs={{0,1},{1,2},{2,3},{3,4},{4,5},{5,6},{6,7},{7,8},{8,9},{9,10},{10,1... | collective-permute-start | bytes 1179656 | tf_op jit(solution)/shard_map/ppermute | solution.py:18
  86.2 3.4 collective-permute-done.6
  89.6 12.7 %collective-permute-done.7 = bf16[1,16,96,128]{3,2,1,0:T(8,128)(2,1)S(1)} collective-permute-done((bf16[1,16,96,128]{3,2,1,0:T(8,128)(2,1)S(1)}, bf16[1,16,96,128]{3,2,1,0:T(8,128)(2,1)S(1)}, u32[]{:S(2)}, u32[]{:S(2)}) %collective-permute-start.7) | collective-permute-done | bytes 393248 | tf_op jit(solution)/shard_map/ppermute | solution.py:20
  102.3 6.8 %fusion.30 = bf16[4,16,96,128]{3,2,1,0:T(8,128)(2,1)S(1)} fusion(f32[4,16,1,128]{3,2,1,0:T(1,128)S(1)} %broadcast_in_dim.163, f32[4,16,95,128]{3,2,1,0:T(8,128)S(1)} %get-tuple-element.32, f32[4,16,95,128]{3,2,1,0:T(8,128)S(1)} %get-tuple-element.31, f32[4,16,1,128]{3,2,1,0:T(1,128)S(1)} %broadcast_in_dim.162, f32[4,1,96,128]{3,2,1,0:T(8,128)S(1)} %broadcast_in_dim.161, ...), kind=kLoop, calls=%fused_computation.44 | loop fusion | flops 17301504 | bytes 16687108 | tf_op jit(solution)/shard_map/convert_element_type | solution.py:79
  110.4 2.1 fusion.48
  112.5 5.5 %collective-permute-start.8 = (bf16[1,16,96,128]{3,2,1,0:T(8,128)(2,1)S(1)}, bf16[1,16,96,128]{3,2,1,0:T(8,128)(2,1)S(1)}, u32[]{:S(2)}, u32[]{:S(2)}) collective-permute-start(bf16[1,16,96,128]{3,2,1,0:T(8,128)(2,1)S(1)} %get-tuple-element.21), channel_id=1, source_target_pairs={{0,1},{1,2},{2,3},{3,4},{4,5},{5,6},{6,7},{7,8},{8,9},{9,10},{10,1... | collective-permute-start | bytes 1179656 | tf_op jit(solution)/shard_map/ppermute | solution.py:18
  120.2 4.5 %collective-permute-done.8 = bf16[1,16,96,128]{3,2,1,0:T(8,128)(2,1)S(1)} collective-permute-done((bf16[1,16,96,128]{3,2,1,0:T(8,128)(2,1)S(1)}, bf16[1,16,96,128]{3,2,1,0:T(8,128)(2,1)S(1)}, u32[]{:S(2)}, u32[]{:S(2)}) %collective-permute-start.8) | collective-permute-done | bytes 393248 | tf_op jit(solution)/shard_map/ppermute | solution.py:18
  124.7 11.6 %collective-permute-done.9 = bf16[1,16,96,128]{3,2,1,0:T(8,128)(2,1)S(1)} collective-permute-done((bf16[1,16,96,128]{3,2,1,0:T(8,128)(2,1)S(1)}, bf16[1,16,96,128]{3,2,1,0:T(8,128)(2,1)S(1)}, u32[]{:S(2)}, u32[]{:S(2)}) %collective-permute-start.9) | collective-permute-done | bytes 393248 | tf_op jit(solution)/shard_map/ppermute | solution.py:20
  136.2 7.6 %fusion.47 = f32[128,128]{1,0:T(8,128)} fusion(bf16[4,16,96,128]{3,2,1,0:T(8,128)(2,1)S(1)} %fusion.30, f32[4,16,95,128]{3,2,1,0:T(8,128)S(1)} %get-tuple-element.26, f32[4,16,95,128]{3,2,1,0:T(8,128)S(1)} %get-tuple-element.25, f32[4,15,96,128]{3,2,1,0:T(8,128)S(1)} %get-tuple-element.24, f32[4,15,96,128]{3,2,1,0:T(8,128)S(1)} %get-tuple-element.23, ...), kind=kOutput, calls=%fused_computation.70 | convolution fusion | flops 216268800 | bytes 14721024 | tf_op jit(solution)/shard_map/dot_general | solution.py:106
  143.8 158.6 %all-reduce.7.cloned.1.call-done = (f32[128,128]{1,0:T(8,128)}, f32[128,128]{1,0:T(8,128)}) async-done(((f32[128,128]{1,0:T(8,128)}, f32[128,128]{1,0:T(8,128)}), (f32[128,128]{1,0:T(8,128)}, f32[128,128]{1,0:T(8,128)})) %all-reduce.7.cloned.1.call-update) | async-done | bytes 131088 | tf_op jit(solution)/shard_map/psum | solution.py:144
  304.4 11.7 %cholesky.36 = f32[128,128]{1,0:T(8,128)S(1)} custom-call(f32[128,128]{1,0:T(8,128)S(1)} %fusion.67), custom_call_target="Cholesky" | custom-call | tf_op jit(solution)/shard_map/jit(cholesky)/cholesky | solution.py:114
  317.5 10.0 %custom-call.25 = f32[1,128,128]{1,2,0:T(8,128)S(1)} custom-call(f32[1,128,128]{2,1,0:T(8,128)S(1)} %fusion.50), custom_call_target="InvertDiagBlocksLowerTriangular" | custom-call | tf_op jit(solution)/shard_map/jit(_cho_solve)/triangular_solve | solution.py:118
  330.5 2.9 cholesky.115
  334.7 2.4 custom-call.20
  340.4 2.9 cholesky.126
  344.6 2.4 custom-call.22
  349.5 2.9 cholesky.137
  353.7 2.4 custom-call.24
  357.7 2.9 cholesky.148
  362.0 2.4 custom-call.26
  366.0 15.6 %all-to-all-start = ((bf16[16,32,384]{2,1,0:T(8,128)(2,1)}), bf16[16,32,384]{2,1,0:T(8,128)(2,1)S(1)}, u32[]{:S(2)}, u32[]{:S(2)}) async-start(bf16[16,32,384]{2,1,0:T(8,128)(2,1)} %fusion.46), calls=%async_computation | async-start | bytes 786432 | tf_op jit(solution)/shard_map/all_to_all | solution.py:154
  381.9 8.1 %all-to-all-done = bf16[16,32,384]{2,1,0:T(8,128)(2,1)S(1)} async-done(((bf16[16,32,384]{2,1,0:T(8,128)(2,1)}), bf16[16,32,384]{2,1,0:T(8,128)(2,1)S(1)}, u32[]{:S(2)}, u32[]{:S(2)}) %all-to-all-start) | async-done | bytes 393248 | tf_op jit(solution)/shard_map/all_to_all | solution.py:154
  (106 shorter events, 42.2 us)
Async XLA Ops:
  6.5 320.9 %copy-start = (f32[1,128,32]{1,2,0:T(8,128)S(1)}, f32[1,128,32]{1,2,0:T(8,128)}, u32[]{:S(2)}) copy-start(f32[1,128,32]{1,2,0:T(8,128)} %param.17) | copy-start | bytes 49156
  6.5 295.9 %all-reduce.7.cloned.1.call-start = ((), (), s32[]{:S(2)}) async-start(), calls=%async_computation.1 | async-start | bytes 262144 | tf_op jit(solution)/shard_map/psum | solution.py:144
  7.9 26.6 %collective-permute-start = (s32[1,16,96]{2,1,0:T(8,128)}, s32[1,16,96]{2,1,0:T(8,128)}, u32[]{:S(2)}, u32[]{:S(2)}) collective-permute-start(s32[1,16,96]{2,1,0:T(8,128)} %get-tuple-element.47), channel_id=1, source_target_pairs={{0,1},{1,2},{2,3},{3,4},{4,5},{5,6},{6,7},{7,8},{8,9},{9,10},{10,1... | collective-permute-start | bytes 18440 | tf_op jit(solution)/shard_map/ppermute | solution.py:18
  14.1 20.4 %collective-permute-start.1 = (s32[1,16,96]{2,1,0:T(8,128)}, s32[1,16,96]{2,1,0:T(8,128)}, u32[]{:S(2)}, u32[]{:S(2)}) collective-permute-start(s32[1,16,96]{2,1,0:T(8,128)} %get-tuple-element.48), channel_id=1, source_target_pairs={{1,0},{2,1},{3,2},{4,3},{5,4},{6,5},{7,6},{8,7},{9,8},{10,9},{11,1... | collective-permute-start | bytes 18440 | tf_op jit(solution)/shard_map/ppermute | solution.py:20
  17.3 21.4 %collective-permute-start.2 = (bf16[1,16,96,128]{3,2,1,0:T(8,128)(2,1)}, bf16[1,16,96,128]{3,2,1,0:T(8,128)(2,1)}, u32[]{:S(2)}, u32[]{:S(2)}) collective-permute-start(bf16[1,16,96,128]{3,2,1,0:T(8,128)(2,1)} %get-tuple-element.39), channel_id=1, source_target_pairs={{0,1},{1,2},{2,3},{3,4},{4,5},{5,6},{6,7},{7,8},{8,9},{9,10},{10,1... | collective-permute-start | bytes 1179656 | tf_op jit(solution)/shard_map/ppermute | solution.py:18
  23.5 15.1 %collective-permute-start.3 = (bf16[1,16,96,128]{3,2,1,0:T(8,128)(2,1)S(1)}, bf16[1,16,96,128]{3,2,1,0:T(8,128)(2,1)}, u32[]{:S(2)}, u32[]{:S(2)}) collective-permute-start(bf16[1,16,96,128]{3,2,1,0:T(8,128)(2,1)S(1)} %get-tuple-element.40), channel_id=1, source_target_pairs={{1,0},{2,1},{3,2},{4,3},{5,4},{6,5},{7,6},{8,7},{9,8},{10,9},{11,1... | collective-permute-start | bytes 1179656 | tf_op jit(solution)/shard_map/ppermute | solution.py:20
  49.9 11.8 %collective-permute-start.4 = (bf16[1,16,96,128]{3,2,1,0:T(8,128)(2,1)S(1)}, bf16[1,16,96,128]{3,2,1,0:T(8,128)(2,1)S(1)}, u32[]{:S(2)}, u32[]{:S(2)}) collective-permute-start(bf16[1,16,96,128]{3,2,1,0:T(8,128)(2,1)S(1)} %get-tuple-element.33), channel_id=1, source_target_pairs={{0,1},{1,2},{2,3},{3,4},{4,5},{5,6},{6,7},{7,8},{8,9},{9,10},{10,1... | collective-permute-start | bytes 1179656 | tf_op jit(solution)/shard_map/ppermute | solution.py:18
  55.6 14.2 %collective-permute-start.5 = (bf16[1,16,96,128]{3,2,1,0:T(8,128)(2,1)S(1)}, bf16[1,16,96,128]{3,2,1,0:T(8,128)(2,1)S(1)}, u32[]{:S(2)}, u32[]{:S(2)}) collective-permute-start(bf16[1,16,96,128]{3,2,1,0:T(8,128)(2,1)S(1)} %get-tuple-element.34), channel_id=1, source_target_pairs={{1,0},{2,1},{3,2},{4,3},{5,4},{6,5},{7,6},{8,7},{9,8},{10,9},{11,1... | collective-permute-start | bytes 1179656 | tf_op jit(solution)/shard_map/ppermute | solution.py:20
  77.9 11.8 %collective-permute-start.6 = (bf16[1,16,96,128]{3,2,1,0:T(8,128)(2,1)S(1)}, bf16[1,16,96,128]{3,2,1,0:T(8,128)(2,1)S(1)}, u32[]{:S(2)}, u32[]{:S(2)}) collective-permute-start(bf16[1,16,96,128]{3,2,1,0:T(8,128)(2,1)S(1)} %get-tuple-element.27), channel_id=1, source_target_pairs={{0,1},{1,2},{2,3},{3,4},{4,5},{5,6},{6,7},{7,8},{8,9},{9,10},{10,1... | collective-permute-start | bytes 1179656 | tf_op jit(solution)/shard_map/ppermute | solution.py:18
  84.1 18.2 %collective-permute-start.7 = (bf16[1,16,96,128]{3,2,1,0:T(8,128)(2,1)S(1)}, bf16[1,16,96,128]{3,2,1,0:T(8,128)(2,1)S(1)}, u32[]{:S(2)}, u32[]{:S(2)}) collective-permute-start(bf16[1,16,96,128]{3,2,1,0:T(8,128)(2,1)S(1)} %get-tuple-element.28), channel_id=1, source_target_pairs={{1,0},{2,1},{3,2},{4,3},{5,4},{6,5},{7,6},{8,7},{9,8},{10,9},{11,1... | collective-permute-start | bytes 1179656 | tf_op jit(solution)/shard_map/ppermute | solution.py:20
  112.5 12.2 %collective-permute-start.8 = (bf16[1,16,96,128]{3,2,1,0:T(8,128)(2,1)S(1)}, bf16[1,16,96,128]{3,2,1,0:T(8,128)(2,1)S(1)}, u32[]{:S(2)}, u32[]{:S(2)}) collective-permute-start(bf16[1,16,96,128]{3,2,1,0:T(8,128)(2,1)S(1)} %get-tuple-element.21), channel_id=1, source_target_pairs={{0,1},{1,2},{2,3},{3,4},{4,5},{5,6},{6,7},{7,8},{8,9},{9,10},{10,1... | collective-permute-start | bytes 1179656 | tf_op jit(solution)/shard_map/ppermute | solution.py:18
  117.9 18.3 %collective-permute-start.9 = (bf16[1,16,96,128]{3,2,1,0:T(8,128)(2,1)S(1)}, bf16[1,16,96,128]{3,2,1,0:T(8,128)(2,1)S(1)}, u32[]{:S(2)}, u32[]{:S(2)}) collective-permute-start(bf16[1,16,96,128]{3,2,1,0:T(8,128)(2,1)S(1)} %get-tuple-element.22), channel_id=1, source_target_pairs={{1,0},{2,1},{3,2},{4,3},{5,4},{6,5},{7,6},{8,7},{9,8},{10,9},{11,1... | collective-permute-start | bytes 1179656 | tf_op jit(solution)/shard_map/ppermute | solution.py:20
  302.5 46.5 %copy-start.1 = (f32[128,128]{1,0:T(8,128)S(1)}, f32[128,128]{1,0:T(8,128)}, u32[]{:S(2)}) copy-start(f32[128,128]{1,0:T(8,128)} %get-tuple-element.6) | copy-start | bytes 196612
  329.0 52.6 %copy-start.2 = (s32[16,16]{1,0:T(8,128)S(1)}, s32[16,16]{1,0:T(8,128)}, u32[]{:S(2)}) copy-start(s32[16,16]{1,0:T(8,128)} %param.18) | copy-start | bytes 3076
  366.0 23.9 %all-to-all-start = ((bf16[16,32,384]{2,1,0:T(8,128)(2,1)}), bf16[16,32,384]{2,1,0:T(8,128)(2,1)S(1)}, u32[]{:S(2)}, u32[]{:S(2)}) async-start(bf16[16,32,384]{2,1,0:T(8,128)(2,1)} %fusion.46), calls=%async_computation | async-start | bytes 786432 | tf_op jit(solution)/shard_map/all_to_all | solution.py:154
Sparse Core Ops, SparseCore 0:
  143.9 158.4 all-reduce.6
where the time goes:
time: 399 us; the launch traced here: 398 us
  waiting for transfers between devices  214 us (54%)
  other arithmetic  80.2 us (20%)
  starting transfers between devices  52.1 us (13%)
  matrix products  20.5 us (5%)
  local copies, waits for them, and re-layouts  16.8 us (4%)
  between operations  14 us (4%)
    psum x1, waiting for transfers between devices, on_device(): mass_sum, stiff_sum = lax.psum((mass_part, stiff_part), 'sub')  159 us
    ppermute x5, waiting for transfers between devices, with_halo(): lax.ppermute(head, axis, [((i + 1) % count, i) for i in range(ends)])  32.3 us
    ppermute x5, starting transfers between devices, with_halo(): lax.ppermute(tail, axis, [(i, (i + 1) % count) for i in range(ends)])  29.8 us
    convert_element_type x3, other arithmetic, relax(): jnp.where(inside[:, None, None, None], updated, jnp.float32(0.0))  23.4 us
    all_to_all x1, starting transfers between devices, on_device(): lax.all_to_all(pieces, 'nbhd', split_axis=0, concat_axis=0, tiled=True)  15.6 us
    ppermute x5, waiting for transfers between devices, with_halo(): lax.ppermute(tail, axis, [(i, (i + 1) % count) for i in range(ends)])  15.1 us
    another operation x12, other arithmetic, subspace(): lower = jnp.linalg.cholesky(inner)  14.4 us
    another operation x3, other arithmetic, subspace(): factor = jnp.linalg.cholesky(stiff_gram)  12.4 us
  transfers between devices with their start and end apart: 12, of which 9 were waited for; matrix products, arithmetic and copies ran while one was open for 4% of the time, Pallas kernels for 0%

commit v1 on v0

--- a/solution.py
+++ b/solution.py
@@ -1,7 +1,13 @@
+import functools
+
 import jax
 import jax.numpy as jnp
 from jax import lax
+from jax.experimental import pallas as pl
+from jax.experimental.pallas import tpu as pltpu
 from jax.sharding import PartitionSpec as P
+
+MESH = pl.DeviceIdType.MESH
 
 SWEEPS = 3
 ITERS = 4
@@ -107,20 +113,185 @@
     return (mass_part, stiff_part)
 
 
-def subspace(mass_sum, stiff_sum, start, cell_count):
-    highest = lax.Precision.HIGHEST
-    mass_gram = mass_sum / cell_count
-    stiff_gram = (stiff_sum + stiff_sum.T) * (0.5 / cell_count)
-    factor = jnp.linalg.cholesky(stiff_gram)
-    mode_block = start
-    for step in range(ITERS):
-        right_side = jnp.dot(mass_gram, mode_block, precision=highest)
-        solved = jax.scipy.linalg.cho_solve((factor, True), right_side)
-        inner = jnp.dot(solved.T, jnp.dot(mass_gram, solved, precision=highest), precision=highest)
+def eliminate_spd(full, size, block):
+    lanes = lax.broadcasted_iota(jnp.int32, (block, size), 1)
+    rows = lax.broadcasted_iota(jnp.int32, (block, size), 0)
+    wide = lax.broadcasted_iota(jnp.int32, (size, size), 1)
+    for first in range(0, size, block):
+        panel = full[first:first + block]
+        signed = jnp.where(lanes < first, -panel, panel) if first else panel
+        for i in range(block):
+            col = first + i
+            column = panel[:, col:col + 1]
+            pivot = 1.0 / panel[i:i + 1, col:col + 1]
+            row = jnp.where(lanes[:1] == col, 1.0, panel[i:i + 1]) * pivot
+            cleared = jnp.where(lanes == col, 0.0, panel)
+            panel = jnp.where(rows == i, row, cleared - column * row)
+        inside = (wide >= first) & (wide < first + block)
+        update = lax.dot_general(
+            signed, panel, (((0,), (0,)), ((), ())),
+            precision=lax.Precision.HIGHEST, preferred_element_type=jnp.float32,
+        )
+        rest = jnp.where(inside, 0.0, full) - update
+        parts = []
+        if first:
+            parts.append(rest[:first])
+        parts.append(panel)
+        if first + block < size:
+            parts.append(rest[first + block:])
+        full = jnp.concatenate(parts, axis=0)
+    return full
+
+
+def normalize(inner, vectors):
+    count = inner.shape[0]
+    rows = lax.broadcasted_iota(jnp.int32, (count, 1), 0)
+    eye = lax.broadcasted_iota(jnp.int32, (count, count), 0) == lax.broadcasted_iota(
+        jnp.int32, (count, count), 1
+    )
+    for i in range(count - 1):
+        factor = inner[:, i:i + 1] * (1.0 / inner[i:i + 1, i:i + 1])
+        factor = jnp.where(rows > i, factor, 0.0)
+        lead, mate = inner[i:i + 1], vectors[i:i + 1]
+        inner = inner - factor * lead
+        vectors = vectors - factor * mate
+    diagonal = jnp.sum(jnp.where(eye, inner, 0.0), axis=1, keepdims=True)
+    return vectors / jnp.sqrt(diagonal)
+
+
+def modes_kernel(
+    snaps_ref, gram_ref, start_ref, corr_ref, out_ref,
+    slots, summed, total, stage, send_sem, recv_sem, send_two, recv_two, send_out, recv_out,
+    *, members, owners, cell_count,
+):
+    me_sub = lax.axis_index("sub")
+    me_nbhd = lax.axis_index("nbhd")
+    size = gram_ref.shape[1]
+    chunk = 2 * size // members
+
+    def sub_at(step):
+        return lax.rem(me_sub + step, members)
+
+    def owner_at(step):
+        return lax.rem(me_nbhd + step, owners)
+
+    barrier = pltpu.get_barrier_semaphore()
+    for step in range(1, members):
+        pl.semaphore_signal(barrier, inc=1, device_id=(me_nbhd, sub_at(step)), device_id_type=MESH)
+    for step in range(1, owners):
+        pl.semaphore_signal(barrier, inc=1, device_id=(owner_at(step), me_sub), device_id_type=MESH)
+    pl.semaphore_wait(barrier, members - 1 + owners - 1)
+
+    def part(owner):
+        return pl.ds(pl.multiple_of(owner * chunk, chunk), chunk)
+
+    copies = []
+    for step in range(1, members):
+        peer = sub_at(step)
+        copy = pltpu.make_async_remote_copy(
+            src_ref=gram_ref.at[part(peer)],
+            dst_ref=slots.at[step],
+            send_sem=send_sem.at[step],
+            recv_sem=recv_sem.at[step],
+            device_id=(me_nbhd, peer),
+            device_id_type=MESH,
+        )
+        copy.start()
+        copies.append(copy)
+    acc = gram_ref[part(me_sub)]
+    for step in range(1, members):
+        copies[step - 1].wait_recv()
+        acc = acc + slots[step]
+    summed[...] = acc
+    total[part(me_sub)] = acc
+    spread = []
+    for step in range(1, members):
+        copy = pltpu.make_async_remote_copy(
+            src_ref=summed,
+            dst_ref=total.at[part(me_sub)],
+            send_sem=send_two.at[step],
+            recv_sem=recv_two.at[step],
+            device_id=(me_nbhd, sub_at(step)),
+            device_id_type=MESH,
+        )
+        copy.start()
+        spread.append(copy)
+    for copy in spread:
+        copy.wait_recv()
+
+    dot = functools.partial(
+        lax.dot_general, precision=lax.Precision.HIGHEST, preferred_element_type=jnp.float32
+    )
+    mass = total[:size] / cell_count
+    stiff = total[size:]
+    stiff = (stiff + stiff.T) * (0.5 / cell_count)
+    inverse = eliminate_spd(stiff, size, 32)
+    step_map = dot(mass, inverse, (((1,), (0,)), ((), ())))
+    both = jnp.concatenate([step_map, dot(step_map, mass, (((1,), (0,)), ((), ())))], axis=1)
+    rows = None
+    for turn in range(ITERS):
+        if turn == 0:
+            pair = dot(start_ref[...], both, (((0,), (0,)), ((), ())))
+        else:
+            pair = dot(rows, both, (((1,), (0,)), ((), ())))
+        solved, image = pair[:, :size], pair[:, size:]
+        inner = dot(solved, image, (((1,), (1,)), ((), ())))
         inner = 0.5 * (inner + inner.T)
-        lower = jnp.linalg.cholesky(inner)
-        mode_block = jax.scipy.linalg.solve_triangular(lower, solved.T, lower=True).T
-    return mode_block
+        rows = normalize(inner, solved)
+    modes = rows.astype(jnp.bfloat16)
+
+    def piece(owner):
+        values = lax.dot_general(
+            modes, snaps_ref[owner], (((1,), (1,)), ((), ())), preferred_element_type=jnp.float32
+        )
+        return (values * corr_ref[me_nbhd, owner].astype(jnp.float32)).astype(jnp.bfloat16)
+
+    leaving = []
+    for step in range(1, owners):
+        owner = owner_at(step)
+        stage[step] = piece(owner)
+        copy = pltpu.make_async_remote_copy(
+            src_ref=stage.at[step],
+            dst_ref=out_ref.at[me_nbhd],
+            send_sem=send_out.at[step],
+            recv_sem=recv_out.at[step],
+            device_id=(owner, me_sub),
+            device_id_type=MESH,
+        )
+        copy.start()
+        leaving.append(copy)
+    out_ref[me_nbhd] = piece(me_nbhd)
+    for copy in leaving:
+        copy.wait_recv()
+    for copy in copies + spread + leaving:
+        copy.wait_send()
+
+
+def modes_and_pieces(snaps, gram, start, corr, members, owners, cell_count):
+    pieces, cells, size = snaps.shape
+    modes = start.shape[1]
+    vmem = pl.BlockSpec(memory_space=pltpu.VMEM)
+    return pl.pallas_call(
+        functools.partial(modes_kernel, members=members, owners=owners, cell_count=cell_count),
+        out_shape=jax.ShapeDtypeStruct((owners, modes, cells), jnp.bfloat16),
+        in_specs=[vmem, vmem, vmem, pl.BlockSpec(memory_space=pltpu.SMEM)],
+        out_specs=vmem,
+        scratch_shapes=[
+            pltpu.VMEM((members, 2 * size // members, size), jnp.float32),
+            pltpu.VMEM((2 * size // members, size), jnp.float32),
+            pltpu.VMEM((2 * size, size), jnp.float32),
+            pltpu.VMEM((owners, modes, cells), jnp.bfloat16),
+            pltpu.SemaphoreType.DMA((members,)),
+            pltpu.SemaphoreType.DMA((members,)),
+            pltpu.SemaphoreType.DMA((members,)),
+            pltpu.SemaphoreType.DMA((members,)),
+            pltpu.SemaphoreType.DMA((owners,)),
+            pltpu.SemaphoreType.DMA((owners,)),
+        ],
+        compiler_params=pltpu.CompilerParams(
+            collective_id=1, has_side_effects=True, vmem_limit_bytes=32 << 20
+        ),
+    )(snaps, gram, start, corr)
 
 
 def on_device(snap_init, channel_map, yface_vals, zface_vals, face_of, start_block, correlation):
@@ -141,19 +312,15 @@
     kappa_local = kappa_edge[1:-1]
     stiff_apply = stiffness(field_edge, kappa_edge, base_plane - 1, plane_count)
     mass_part, stiff_part = gram_terms(snapshots, kappa_local, stiff_apply)
-    mass_sum, stiff_sum = lax.psum((mass_part, stiff_part), "sub")
     cell_count = float(plane_count * snapshots.shape[1] * snapshots.shape[2])
-    mode_block = subspace(mass_sum, stiff_sum, start_block[0], cell_count)
     owner_count = lax.axis_size("nbhd")
     width = snapshots.shape[-1]
     piece_cells = snapshots.size // width // owner_count
     blocks = snapshots.reshape(owner_count, piece_cells, width)
-    pieces = jnp.einsum(
-        "pcs,sm->pmc", blocks, mode_block.astype(jnp.bfloat16), preferred_element_type=jnp.float32
-    ).astype(jnp.bfloat16)
-    received = lax.all_to_all(pieces, "nbhd", split_axis=0, concat_axis=0, tiled=True)
-    column = lax.dynamic_slice_in_dim(correlation, lax.axis_index("nbhd"), 1, axis=1)[:, 0]
-    result = received * column.astype(jnp.bfloat16)[:, None, None]
+    result = modes_and_pieces(
+        blocks, jnp.concatenate([mass_part, stiff_part]), start_block[0], correlation,
+        lax.axis_size("sub"), owner_count, cell_count,
+    )
     return result[None, None]
 
 

time: 399 us -> 202 us (0.51)
  waiting for transfers between devices: 214 us -> 49.8 us
  Pallas kernels: 0 us -> 66.5 us
  other arithmetic: 80.2 us -> 25.6 us
  starting transfers between devices: 52.1 us -> 35.2 us
  between operations: 14 us -> 0.36 us
  matrix products: 20.5 us -> 8.96 us
    psum x1 -> x0, waiting for transfers between devices: 159 us -> none  [on_device(): mass_sum, stiff_sum = lax.psum((mass_part, stiff_part), 'sub')]
    pallas_call x0 -> x1, Pallas kernels: none -> 66.5 us  [modes_and_pieces(): pl.pallas_call(functools.partial(modes_kernel, members=members, owners=ow...]
    another operation x25 -> x0, other arithmetic: 49.8 us -> none  [the longest x12 14.4 us: subspace(): lower = jnp.linalg.cholesky(inner)]
    all_to_all x1 -> x0, starting transfers between devices: 15.6 us -> none  [on_device(): lax.all_to_all(pieces, 'nbhd', split_axis=0, concat_axis=0, tiled=True)]
    all_to_all x1 -> x0, waiting for transfers between devices: 8.08 us -> none  [on_device(): lax.all_to_all(pieces, 'nbhd', split_axis=0, concat_axis=0, tiled=True)]
    dot_general x13 -> x0, matrix products: 7.81 us -> none  [the longest x4 3.3 us: subspace(): right_side = jnp.dot(mass_gram, mode_block, precision=highest)]
  transfers between devices with their start and end apart: 12 -> 10, of which waited for: 9 -> 7; matrix products, arithmetic and copies ran while one was open for 4% -> 7% of each run, Pallas kernels for 0% -> 0%
where the time goes in v1:
time: 202 us
  Pallas kernels  66.5 us (33%)
  waiting for transfers between devices  49.8 us (25%)
  starting transfers between devices  35.2 us (17%)
  other arithmetic  25.6 us (13%)
  local copies, waits for them, and re-layouts  15.4 us (8%)
  matrix products  8.96 us (4%)
    pallas_call x1, Pallas kernels, modes_and_pieces(): pl.pallas_call(functools.partial(modes_kernel, members=members, owners=ow...  66.5 us
    ppermute x5, waiting for transfers between devices, with_halo(): lax.ppermute(head, axis, [((i + 1) % count, i) for i in range(ends)])  33 us
    ppermute x5, starting transfers between devices, with_halo(): lax.ppermute(tail, axis, [(i, (i + 1) % count) for i in range(ends)])  28.6 us
    convert_element_type x3, other arithmetic, relax(): jnp.where(inside[:, None, None, None], updated, jnp.float32(0.0))  23.4 us
    ppermute x5, waiting for transfers between devices, with_halo(): lax.ppermute(tail, axis, [(i, (i + 1) % count) for i in range(ends)])  16.9 us
    dot_general x1, matrix products, gram_terms(): lax.dot_general(flat, stiff_flat, dims, preferred_element_type=jnp.float32)  7.5 us
    ppermute x5, starting transfers between devices, with_halo(): lax.ppermute(head, axis, [((i + 1) % count, i) for i in range(ends)])  6.63 us
    slice x4, local copies, waits for them, and re-layouts, face_terms(): middle[:, :, :-1]  5.93 us
  transfers between devices with their start and end apart: 10, of which 7 were waited for; matrix products, arithmetic and copies ran while one was open for 7% of the time, Pallas kernels for 0%

profile of v1, /device:TPU:1, one launch (start us, length us, event | category | flops | bytes accessed | tf_op | source)
XLA Modules:
  0.0 201.9 jit_solution(1133299861446547789)
XLA Ops:
  0.7 5.6 %collective-permute-start = (s32[1,16,96]{2,1,0:T(8,128)S(1)}, s32[1,16,96]{2,1,0:T(8,128)S(1)}, u32[]{:S(2)}, u32[]{:S(2)}) collective-permute-start(s32[1,16,96]{2,1,0:T(8,128)S(1)} %get-tuple-element.42), channel_id=1, source_target_pairs={{0,1},{1,2},{2,3},{3,4},{4,5},{5,6},{6,7},{7,8},{8,9},{9,10},{10,1... | collective-permute-start | bytes 18440 | tf_op jit(solution)/shard_map/ppermute | solution.py:24
  6.4 1.3 collective-permute-start.1
  7.7 2.0 %slice_bitcast_fusion.1 = (bf16[1,16,96,128]{3,2,1,0:T(8,128)(2,1)}, bf16[1,16,96,128]{3,2,1,0:T(8,128)(2,1)}) fusion(bf16[1,4,16,96,128]{4,3,2,1,0:T(8,128)(2,1)} %param.7), kind=kLoop, calls=%fused_computation.71 | loop fusion | bytes 1572864 | tf_op jit(solution)/shard_map/slice | solution.py:21
  9.7 6.3 %collective-permute-start.2 = (bf16[1,16,96,128]{3,2,1,0:T(8,128)(2,1)}, bf16[1,16,96,128]{3,2,1,0:T(8,128)(2,1)}, u32[]{:S(2)}, u32[]{:S(2)}) collective-permute-start(bf16[1,16,96,128]{3,2,1,0:T(8,128)(2,1)} %get-tuple-element.34), channel_id=1, source_target_pairs={{0,1},{1,2},{2,3},{3,4},{4,5},{5,6},{6,7},{7,8},{8,9},{9,10},{10,1... | collective-permute-start | bytes 1179656 | tf_op jit(solution)/shard_map/ppermute | solution.py:24
  16.0 1.3 collective-permute-start.3
  17.3 1.8 bitcast_convert_fusion
  19.1 2.4 %fusion.57 = (f32[4,16,95,128]{3,2,1,0:T(8,128)S(1)}, f32[4,16,95,128]{3,2,1,0:T(8,128)}) fusion(f32[4,16,96,128]{3,2,1,0:T(8,128)S(1)} %bitcast_convert_fusion), kind=kLoop, calls=%fused_computation.106 | loop fusion | bytes 12451840 | tf_op jit(solution)/shard_map/slice | solution.py:61
  21.5 3.3 %fusion.56 = (f32[4,15,96,128]{3,2,1,0:T(8,128)}, f32[4,15,96,128]{3,2,1,0:T(8,128)}) fusion(f32[4,16,96,128]{3,2,1,0:T(8,128)S(1)} %bitcast_convert_fusion), kind=kLoop, calls=%fused_computation.105 | loop fusion | bytes 11796480 | tf_op jit(solution)/shard_map/slice | solution.py:55
  25.4 5.7 %collective-permute-done.2 = bf16[1,16,96,128]{3,2,1,0:T(8,128)(2,1)} collective-permute-done((bf16[1,16,96,128]{3,2,1,0:T(8,128)(2,1)}, bf16[1,16,96,128]{3,2,1,0:T(8,128)(2,1)}, u32[]{:S(2)}, u32[]{:S(2)}) %collective-permute-start.2) | collective-permute-done | bytes 393248 | tf_op jit(solution)/shard_map/ppermute | solution.py:24
  31.2 9.9 %fusion.32 = bf16[4,16,96,128]{3,2,1,0:T(8,128)(2,1)S(1)} fusion(f32[4,16,1,128]{3,2,1,0:T(1,128)S(1)} %broadcast_in_dim.159, f32[4,16,95,128]{3,2,1,0:T(8,128)} %get-tuple-element.15, f32[4,16,95,128]{3,2,1,0:T(8,128)S(1)} %get-tuple-element.14, f32[4,16,1,128]{3,2,1,0:T(1,128)S(1)} %broadcast_in_dim.158, f32[4,1,96,128]{3,2,1,0:T(8,128)S(1)} %broadcast_in_dim.157, ...), kind=kLoop, calls=%fused_computation.46 | loop fusion | flops 17301504 | bytes 16687108 | tf_op jit(solution)/shard_map/convert_element_type | solution.py:85
  41.1 1.2 fusion.66
  42.4 5.6 %collective-permute-start.4 = (bf16[1,16,96,128]{3,2,1,0:T(8,128)(2,1)S(1)}, bf16[1,16,96,128]{3,2,1,0:T(8,128)(2,1)S(1)}, u32[]{:S(2)}, u32[]{:S(2)}) collective-permute-start(bf16[1,16,96,128]{3,2,1,0:T(8,128)(2,1)S(1)} %get-tuple-element.28), channel_id=1, source_target_pairs={{0,1},{1,2},{2,3},{3,4},{4,5},{5,6},{6,7},{7,8},{8,9},{9,10},{10,1... | collective-permute-start | bytes 1179656 | tf_op jit(solution)/shard_map/ppermute | solution.py:24
  48.0 1.3 collective-permute-start.5
  49.3 0.7 fusion.65
  50.1 4.2 %collective-permute-done.4 = bf16[1,16,96,128]{3,2,1,0:T(8,128)(2,1)S(1)} collective-permute-done((bf16[1,16,96,128]{3,2,1,0:T(8,128)(2,1)S(1)}, bf16[1,16,96,128]{3,2,1,0:T(8,128)(2,1)S(1)}, u32[]{:S(2)}, u32[]{:S(2)}) %collective-permute-start.4) | collective-permute-done | bytes 393248 | tf_op jit(solution)/shard_map/ppermute | solution.py:24
  54.2 9.2 %collective-permute-done.5 = bf16[1,16,96,128]{3,2,1,0:T(8,128)(2,1)S(1)} collective-permute-done((bf16[1,16,96,128]{3,2,1,0:T(8,128)(2,1)S(1)}, bf16[1,16,96,128]{3,2,1,0:T(8,128)(2,1)S(1)}, u32[]{:S(2)}, u32[]{:S(2)}) %collective-permute-start.5) | collective-permute-done | bytes 393248 | tf_op jit(solution)/shard_map/ppermute | solution.py:26
  63.4 6.8 %fusion.31 = bf16[4,16,96,128]{3,2,1,0:T(8,128)(2,1)S(1)} fusion(f32[4,16,1,128]{3,2,1,0:T(1,128)S(1)} %broadcast_in_dim.159, f32[4,16,95,128]{3,2,1,0:T(8,128)S(1)} %get-tuple-element.33, f32[4,16,95,128]{3,2,1,0:T(8,128)S(1)} %get-tuple-element.32, f32[4,16,1,128]{3,2,1,0:T(1,128)S(1)} %broadcast_in_dim.158, f32[4,1,96,128]{3,2,1,0:T(8,128)S(1)} %broadcast_in_dim.157, ...), kind=kLoop, calls=%fused_computation.45 | loop fusion | flops 17301504 | bytes 16687108 | tf_op jit(solution)/shard_map/convert_element_type | solution.py:85
  70.2 1.2 fusion.63
  71.5 5.6 %collective-permute-start.6 = (bf16[1,16,96,128]{3,2,1,0:T(8,128)(2,1)S(1)}, bf16[1,16,96,128]{3,2,1,0:T(8,128)(2,1)S(1)}, u32[]{:S(2)}, u32[]{:S(2)}) collective-permute-start(bf16[1,16,96,128]{3,2,1,0:T(8,128)(2,1)S(1)} %get-tuple-element.22), channel_id=1, source_target_pairs={{0,1},{1,2},{2,3},{3,4},{4,5},{5,6},{6,7},{7,8},{8,9},{9,10},{10,1... | collective-permute-start | bytes 1179656 | tf_op jit(solution)/shard_map/ppermute | solution.py:24
  77.1 1.3 collective-permute-start.7
  79.2 4.0 %collective-permute-done.6 = bf16[1,16,96,128]{3,2,1,0:T(8,128)(2,1)S(1)} collective-permute-done((bf16[1,16,96,128]{3,2,1,0:T(8,128)(2,1)S(1)}, bf16[1,16,96,128]{3,2,1,0:T(8,128)(2,1)S(1)}, u32[]{:S(2)}, u32[]{:S(2)}) %collective-permute-start.6) | collective-permute-done | bytes 393248 | tf_op jit(solution)/shard_map/ppermute | solution.py:24
  83.2 12.2 %collective-permute-done.7 = bf16[1,16,96,128]{3,2,1,0:T(8,128)(2,1)S(1)} collective-permute-done((bf16[1,16,96,128]{3,2,1,0:T(8,128)(2,1)S(1)}, bf16[1,16,96,128]{3,2,1,0:T(8,128)(2,1)S(1)}, u32[]{:S(2)}, u32[]{:S(2)}) %collective-permute-start.7) | collective-permute-done | bytes 393248 | tf_op jit(solution)/shard_map/ppermute | solution.py:26
  95.3 6.8 %fusion.30 = bf16[4,16,96,128]{3,2,1,0:T(8,128)(2,1)S(1)} fusion(f32[4,16,1,128]{3,2,1,0:T(1,128)S(1)} %broadcast_in_dim.159, f32[4,16,95,128]{3,2,1,0:T(8,128)S(1)} %get-tuple-element.27, f32[4,16,95,128]{3,2,1,0:T(8,128)S(1)} %get-tuple-element.26, f32[4,16,1,128]{3,2,1,0:T(1,128)S(1)} %broadcast_in_dim.158, f32[4,1,96,128]{3,2,1,0:T(8,128)S(1)} %broadcast_in_dim.157, ...), kind=kLoop, calls=%fused_computation.44 | loop fusion | flops 17301504 | bytes 16687108 | tf_op jit(solution)/shard_map/convert_element_type | solution.py:85
  102.1 1.2 fusion.60
  103.3 5.5 %collective-permute-start.8 = (bf16[1,16,96,128]{3,2,1,0:T(8,128)(2,1)S(1)}, bf16[1,16,96,128]{3,2,1,0:T(8,128)(2,1)S(1)}, u32[]{:S(2)}, u32[]{:S(2)}) collective-permute-start(bf16[1,16,96,128]{3,2,1,0:T(8,128)(2,1)S(1)} %get-tuple-element.16), channel_id=1, source_target_pairs={{0,1},{1,2},{2,3},{3,4},{4,5},{5,6},{6,7},{7,8},{8,9},{9,10},{10,1... | collective-permute-start | bytes 1179656 | tf_op jit(solution)/shard_map/ppermute | solution.py:24
  108.8 1.5 collective-permute-start.9
  110.3 1.5 fusion.47
  112.5 3.0 %collective-permute-done.8 = bf16[1,16,96,128]{3,2,1,0:T(8,128)(2,1)S(1)} collective-permute-done((bf16[1,16,96,128]{3,2,1,0:T(8,128)(2,1)S(1)}, bf16[1,16,96,128]{3,2,1,0:T(8,128)(2,1)S(1)}, u32[]{:S(2)}, u32[]{:S(2)}) %collective-permute-start.8) | collective-permute-done | bytes 393248 | tf_op jit(solution)/shard_map/ppermute | solution.py:24
  115.5 11.6 %collective-permute-done.9 = bf16[1,16,96,128]{3,2,1,0:T(8,128)(2,1)S(1)} collective-permute-done((bf16[1,16,96,128]{3,2,1,0:T(8,128)(2,1)S(1)}, bf16[1,16,96,128]{3,2,1,0:T(8,128)(2,1)S(1)}, u32[]{:S(2)}, u32[]{:S(2)}) %collective-permute-start.9) | collective-permute-done | bytes 393248 | tf_op jit(solution)/shard_map/ppermute | solution.py:26
  127.1 7.5 %fusion.46 = f32[128,128]{1,0:T(8,128)S(1)} fusion(bf16[4,16,96,128]{3,2,1,0:T(8,128)(2,1)S(1)} %fusion.30, f32[4,16,95,128]{3,2,1,0:T(8,128)S(1)} %get-tuple-element.21, f32[4,16,95,128]{3,2,1,0:T(8,128)S(1)} %get-tuple-element.20, f32[4,15,96,128]{3,2,1,0:T(8,128)S(1)} %get-tuple-element.19, f32[4,15,96,128]{3,2,1,0:T(8,128)S(1)} %get-tuple-element.18, ...), kind=kOutput, calls=%fused_computation.68 | convolution fusion | flops 216268800 | bytes 14721024 | tf_op jit(solution)/shard_map/dot_general | solution.py:112
  134.6 66.5 %shard_map.73 = bf16[16,32,384]{2,1,0:T(8,128)(2,1)S(1)} custom-call(bf16[16,384,128]{2,1,0:T(8,128)(2,1)S(1)} %bitcast.40, f32[256,128]{1,0:T(8,128)S(1)} %pad_maximum_fusion.21.gram_ref, f32[128,32]{1,0:T(8,128)S(1)} %bitcast.42, s32[16,16]{1,0:T(8,128)S(1)} %copy-done), custom_call_target="tpu_custom_call" | custom-call | tf_op jit(solution)/shard_map/pallas_call | solution.py:274
  201.1 0.7 copy.12
  (39 shorter events, 3.0 us)
Async XLA Ops:
  0.7 24.3 %collective-permute-start = (s32[1,16,96]{2,1,0:T(8,128)S(1)}, s32[1,16,96]{2,1,0:T(8,128)S(1)}, u32[]{:S(2)}, u32[]{:S(2)}) collective-permute-start(s32[1,16,96]{2,1,0:T(8,128)S(1)} %get-tuple-element.42), channel_id=1, source_target_pairs={{0,1},{1,2},{2,3},{3,4},{4,5},{5,6},{6,7},{7,8},{8,9},{9,10},{10,1... | collective-permute-start | bytes 18440 | tf_op jit(solution)/shard_map/ppermute | solution.py:24
  6.4 18.6 %collective-permute-start.1 = (s32[1,16,96]{2,1,0:T(8,128)S(1)}, s32[1,16,96]{2,1,0:T(8,128)S(1)}, u32[]{:S(2)}, u32[]{:S(2)}) collective-permute-start(s32[1,16,96]{2,1,0:T(8,128)S(1)} %get-tuple-element.43), channel_id=1, source_target_pairs={{1,0},{2,1},{3,2},{4,3},{5,4},{6,5},{7,6},{8,7},{9,8},{10,9},{11,1... | collective-permute-start | bytes 18440 | tf_op jit(solution)/shard_map/ppermute | solution.py:26
  9.7 21.4 %collective-permute-start.2 = (bf16[1,16,96,128]{3,2,1,0:T(8,128)(2,1)}, bf16[1,16,96,128]{3,2,1,0:T(8,128)(2,1)}, u32[]{:S(2)}, u32[]{:S(2)}) collective-permute-start(bf16[1,16,96,128]{3,2,1,0:T(8,128)(2,1)} %get-tuple-element.34), channel_id=1, source_target_pairs={{0,1},{1,2},{2,3},{3,4},{4,5},{5,6},{6,7},{7,8},{8,9},{9,10},{10,1... | collective-permute-start | bytes 1179656 | tf_op jit(solution)/shard_map/ppermute | solution.py:24
  16.0 15.1 %collective-permute-start.3 = (bf16[1,16,96,128]{3,2,1,0:T(8,128)(2,1)}, bf16[1,16,96,128]{3,2,1,0:T(8,128)(2,1)}, u32[]{:S(2)}, u32[]{:S(2)}) collective-permute-start(bf16[1,16,96,128]{3,2,1,0:T(8,128)(2,1)} %get-tuple-element.35), channel_id=1, source_target_pairs={{1,0},{2,1},{3,2},{4,3},{5,4},{6,5},{7,6},{8,7},{9,8},{10,9},{11,1... | collective-permute-start | bytes 1179656 | tf_op jit(solution)/shard_map/ppermute | solution.py:26
  21.4 3.3 %copy-start.5 = (s32[1,128]{1,0:T(1,128)S(1)}, s32[1,128]{1,0:T(1,128)}, u32[]{:S(2)}) copy-start(s32[1,128]{1,0:T(1,128)} %param.11) | copy-start | bytes 1540
  21.4 3.3 %copy-start.2 = (bf16[1,96,128]{2,1,0:T(8,128)(2,1)S(1)}, bf16[1,96,128]{2,1,0:T(8,128)(2,1)}, u32[]{:S(2)}) copy-start(bf16[1,96,128]{2,1,0:T(8,128)(2,1)} %param.9) | copy-start | bytes 73732
  21.4 3.3 %copy-start.4 = (bf16[1,16,128]{2,1,0:T(8,128)(2,1)S(1)}, bf16[1,16,128]{2,1,0:T(8,128)(2,1)}, u32[]{:S(2)}) copy-start(bf16[1,16,128]{2,1,0:T(8,128)(2,1)} %param.10) | copy-start | bytes 12292
  21.5 3.4 %copy-start.3 = (f32[1,128,32]{1,2,0:T(8,128)S(1)}, f32[1,128,32]{1,2,0:T(8,128)}, u32[]{:S(2)}) copy-start(f32[1,128,32]{1,2,0:T(8,128)} %param.12) | copy-start | bytes 49156
  21.5 3.6 %copy-start.1 = (s32[1,4,16,96]{3,2,1,0:T(8,128)S(1)}, s32[1,4,16,96]{3,2,1,0:T(8,128)}, u32[]{:S(2)}) copy-start(s32[1,4,16,96]{3,2,1,0:T(8,128)} %param.8) | copy-start | bytes 73732
  42.4 11.8 %collective-permute-start.4 = (bf16[1,16,96,128]{3,2,1,0:T(8,128)(2,1)S(1)}, bf16[1,16,96,128]{3,2,1,0:T(8,128)(2,1)S(1)}, u32[]{:S(2)}, u32[]{:S(2)}) collective-permute-start(bf16[1,16,96,128]{3,2,1,0:T(8,128)(2,1)S(1)} %get-tuple-element.28), channel_id=1, source_target_pairs={{0,1},{1,2},{2,3},{3,4},{4,5},{5,6},{6,7},{7,8},{8,9},{9,10},{10,1... | collective-permute-start | bytes 1179656 | tf_op jit(solution)/shard_map/ppermute | solution.py:24
  48.0 15.4 %collective-permute-start.5 = (bf16[1,16,96,128]{3,2,1,0:T(8,128)(2,1)S(1)}, bf16[1,16,96,128]{3,2,1,0:T(8,128)(2,1)S(1)}, u32[]{:S(2)}, u32[]{:S(2)}) collective-permute-start(bf16[1,16,96,128]{3,2,1,0:T(8,128)(2,1)S(1)} %get-tuple-element.29), channel_id=1, source_target_pairs={{1,0},{2,1},{3,2},{4,3},{5,4},{6,5},{7,6},{8,7},{9,8},{10,9},{11,1... | collective-permute-start | bytes 1179656 | tf_op jit(solution)/shard_map/ppermute | solution.py:26
  71.5 11.7 %collective-permute-start.6 = (bf16[1,16,96,128]{3,2,1,0:T(8,128)(2,1)S(1)}, bf16[1,16,96,128]{3,2,1,0:T(8,128)(2,1)S(1)}, u32[]{:S(2)}, u32[]{:S(2)}) collective-permute-start(bf16[1,16,96,128]{3,2,1,0:T(8,128)(2,1)S(1)} %get-tuple-element.22), channel_id=1, source_target_pairs={{0,1},{1,2},{2,3},{3,4},{4,5},{5,6},{6,7},{7,8},{8,9},{9,10},{10,1... | collective-permute-start | bytes 1179656 | tf_op jit(solution)/shard_map/ppermute | solution.py:24
  77.1 18.2 %collective-permute-start.7 = (bf16[1,16,96,128]{3,2,1,0:T(8,128)(2,1)S(1)}, bf16[1,16,96,128]{3,2,1,0:T(8,128)(2,1)S(1)}, u32[]{:S(2)}, u32[]{:S(2)}) collective-permute-start(bf16[1,16,96,128]{3,2,1,0:T(8,128)(2,1)S(1)} %get-tuple-element.23), channel_id=1, source_target_pairs={{1,0},{2,1},{3,2},{4,3},{5,4},{6,5},{7,6},{8,7},{9,8},{10,9},{11,1... | collective-permute-start | bytes 1179656 | tf_op jit(solution)/shard_map/ppermute | solution.py:26
  103.3 12.2 %collective-permute-start.8 = (bf16[1,16,96,128]{3,2,1,0:T(8,128)(2,1)S(1)}, bf16[1,16,96,128]{3,2,1,0:T(8,128)(2,1)S(1)}, u32[]{:S(2)}, u32[]{:S(2)}) collective-permute-start(bf16[1,16,96,128]{3,2,1,0:T(8,128)(2,1)S(1)} %get-tuple-element.16), channel_id=1, source_target_pairs={{0,1},{1,2},{2,3},{3,4},{4,5},{5,6},{6,7},{7,8},{8,9},{9,10},{10,1... | collective-permute-start | bytes 1179656 | tf_op jit(solution)/shard_map/ppermute | solution.py:24
  108.8 18.3 %collective-permute-start.9 = (bf16[1,16,96,128]{3,2,1,0:T(8,128)(2,1)S(1)}, bf16[1,16,96,128]{3,2,1,0:T(8,128)(2,1)S(1)}, u32[]{:S(2)}, u32[]{:S(2)}) collective-permute-start(bf16[1,16,96,128]{3,2,1,0:T(8,128)(2,1)S(1)} %get-tuple-element.17), channel_id=1, source_target_pairs={{1,0},{2,1},{3,2},{4,3},{5,4},{6,5},{7,6},{8,7},{9,8},{10,9},{11,1... | collective-permute-start | bytes 1179656 | tf_op jit(solution)/shard_map/ppermute | solution.py:26
  127.1 7.5 %copy-start = (s32[16,16]{1,0:T(8,128)S(1)}, s32[16,16]{1,0:T(8,128)}, u32[]{:S(2)}) copy-start(s32[16,16]{1,0:T(8,128)} %corr_ref.1) | copy-start | bytes 3076

commit v2 on v1

v2 whole, which is shorter than its diff:
```python
import functools

import jax
import jax.numpy as jnp
from jax import lax
from jax.experimental import pallas as pl
from jax.experimental.pallas import tpu as pltpu
from jax.sharding import PartitionSpec as P

MESH = pl.DeviceIdType.MESH

SWEEPS = 3
ITERS = 4


def harmonic(left_k, right_k):
    return 2.0 * left_k * right_k / (left_k + right_k)


def relax_kernel(
    snap_ref, class_ref, yface_ref, zface_ref, face_ref, state_ref, gram_ref,
    field, coef, compact, kappa, ghost_z, early, swap, zland, yland, rhs,
    class_pair, class_low, class_high,
    swap_send, swap_recv, z_send, z_recv, y_send, y_recv, class_send, class_recv,
    *, members,
):
    me_nbhd = lax.axis_index("nbhd")
    me = lax.axis_index("sub")
    half = lax.rem(me, 2)
    tower = me // 2
    towers = members // 2
    own, rows_all, depth, width = snap_ref.shape
    both = 2 * own
    rows = rows_all // 2
    top = both + 1
    base = 8
    inner = pl.ds(base, depth)

    def at(sub):
        return (me_nbhd, lax.rem(sub + members, members))

    partner = at(me + 1 - 2 * half)
    cross = at(me - 1 + 2 * half)
    lower = at(me - 2)
    upper = at(me + 2)

    def remote(src, dst, send, recv, device):
        return pltpu.make_async_remote_copy(
            src_ref=src, dst_ref=dst, send_sem=send, recv_sem=recv,
            device_id=device, device_id_type=MESH,
        )

    barrier = pltpu.get_barrier_semaphore()
    for device in (partner, cross, lower, upper):
        pl.semaphore_signal(barrier, inc=1, device_id=device, device_id_type=MESH)
    pl.semaphore_wait(barrier, 4)

    class_copies = [
        remote(class_ref, class_pair, class_send.at[0], class_recv.at[0], partner),
    ]
    class_copies[0].start()
    class_other = []

    def class_sends(plane, land, slot, devices):
        made = []
        for place, device in enumerate(devices):
            made.append(remote(
                class_ref.at[plane], land, class_send.at[1 + place], class_recv.at[slot], device
            ))
        return made

    @pl.when(half == 0)
    def _():
        for copy in class_sends(0, class_high, 2, (lower, cross)):
            copy.start()

    @pl.when(half == 1)
    def _():
        for copy in class_sends(own - 1, class_low, 1, (upper, cross)):
            copy.start()

    order = [0] + list(range(own - 1, 0, -1))
    swaps = []
    for turn, q in enumerate(order):
        plane = q + half * (own - 1 - 2 * q)
        copy = remote(
            snap_ref.at[plane, pl.ds((rows - 1) * (1 - half), rows + 1)],
            swap.at[turn], swap_send.at[turn], swap_recv.at[turn], partner,
        )
        copy.start()
        swaps.append(copy)

    @pl.when(half == 0)
    def _():
        remote(
            snap_ref.at[0, pl.ds(0, rows)], zland.at[0, 1], z_send.at[0, 0], z_recv.at[0, 1], lower
        ).start()

    @pl.when(half == 1)
    def _():
        remote(
            snap_ref.at[own - 1, pl.ds(rows, rows)], zland.at[0, 0], z_send.at[0, 1],
            z_recv.at[0, 0], upper
        ).start()

    shift = 1 - half

    def fill_own(p, _):
        def fill(r, _):
            field[0, 1 + own * half + p, shift + r, inner, :] = snap_ref[
                p, (rows - 1) * half + r
            ].astype(jnp.float32)
            return 0
        return lax.fori_loop(0, rows + 1, fill, 0)

    lax.fori_loop(0, own, fill_own, 0)

    face = face_ref[...]

    def pick(side):
        return jnp.where(face == side, 1.0, 0.0)

    side_y = jnp.where(half == 0, pick(0), pick(1))
    ghost_y = yface_ref[...].astype(jnp.float32) * side_y
    zface = zface_ref[...].astype(jnp.float32)
    ghost_z[0] = zface * pick(2)
    ghost_z[1] = zface * pick(3)

    def set_ghosts(p, _):
        for buf in range(2):
            field[buf, p + 1, (rows + 1) * half, inner, :] = ghost_y

            def one(y, _):
                field[buf, p + 1, y + 1, pl.ds(base - 1, 1), :] = ghost_z[0, pl.ds(rows * half + y, 1), :]
                field[buf, p + 1, y + 1, pl.ds(base + depth, 1), :] = ghost_z[1, pl.ds(rows * half + y, 1), :]
                return 0

            lax.fori_loop(0, rows, one, 0)
        return 0

    lax.fori_loop(0, both, set_ghosts, 0)

    def to_kappa(classes):
        return jnp.left_shift(1, 2 * classes).astype(jnp.float32)

    def land(slot, ref):
        remote(ref, ref, class_send.at[0], class_recv.at[slot], partner).wait_recv()

    land(0, class_pair)
    land(1, class_low)
    land(2, class_high)
    kappa[0] = to_kappa(class_low[...])
    kappa[top] = to_kappa(class_high[...])
    for p in range(own):
        kappa[1 + own * half + p] = to_kappa(class_ref[p])
        kappa[1 + own * (1 - half) + p] = to_kappa(class_pair[p])

    def coefficients(p, _):
        centre = kappa[p + 1]
        has_low = jnp.logical_or(tower > 0, p > 0)
        has_high = jnp.logical_or(tower < towers - 1, p < both - 1)
        face_low = harmonic(centre, kappa[p])
        face_high = harmonic(centre, kappa[p + 2])
        x_lower = jnp.where(has_low, face_low, centre)
        x_upper = jnp.where(has_high, face_high, centre)
        y_inner = harmonic(centre[1:], centre[:-1])
        y_lower = jnp.concatenate([centre[:1], y_inner], axis=0)
        y_upper = jnp.concatenate([y_inner, centre[-1:]], axis=0)
        z_inner = harmonic(centre[:, 1:], centre[:, :-1])
        z_lower = jnp.concatenate([centre[:, :1], z_inner], axis=1)
        z_upper = jnp.concatenate([z_inner, centre[:, -1:]], axis=1)
        denom = x_lower + x_upper + y_lower + y_upper + z_lower + z_upper
        inverse = 1.0 / denom
        compact[0] = jnp.where(has_low, face_low, 0.0) * inverse
        compact[1] = jnp.where(has_high, face_high, 0.0) * inverse
        compact[2] = y_lower * inverse
        compact[3] = y_upper * inverse
        compact[4] = z_lower * inverse
        compact[5] = z_upper * inverse
        compact[6] = denom
        compact[7] = centre * (1.0 / 16.0)
        first = pl.multiple_of(rows * half, rows)
        for kind in range(8):
            turned = compact[kind, pl.ds(first, rows), :].T
            for y in range(rows):
                coef[kind, p, y] = jnp.broadcast_to(turned[:, y:y + 1], (depth, width))
        return 0

    lax.fori_loop(0, both, coefficients, 0)

    def row(sweep, p, y):
        src, dst = (sweep + 1) % 2, sweep % 2
        c = [coef.at[kind, p - 1, y - 1] for kind in range(6)]
        value = c[0][...] * field[src, p - 1, y, inner, :]
        value += c[1][...] * field[src, p + 1, y, inner, :]
        value += c[2][...] * field[src, p, y - 1, inner, :]
        value += c[3][...] * field[src, p, y + 1, inner, :]
        value += c[4][...] * field[src, p, y, pl.ds(base - 1, depth), :]
        value += c[5][...] * field[src, p, y, pl.ds(base + 1, depth), :]
        low = value.astype(jnp.bfloat16)
        field[dst, p, y, inner, :] = low.astype(jnp.float32)
        if sweep < SWEEPS:
            early[sweep - 1, p - 1, y - 1] = low
        else:
            state_ref[p - 1, y - 1] = low
            field[dst, p, y, pl.ds(base + depth, 1), :] = jnp.zeros((1, width), jnp.float32)

    def line(sweep, p, first, count):
        def body(i, _):
            row(sweep, p, first + i)
            return 0
        lax.fori_loop(0, count, body, 0)

    def fill_z(buf, round_no, side):
        remote(
            zland.at[round_no, side], zland.at[round_no, side], z_send.at[round_no, side],
            z_recv.at[round_no, side], lower,
        ).wait_recv()

        def fill(y, _):
            field[buf, top * side, y + 1, inner, :] = zland[round_no, side, y].astype(jnp.float32)
            return 0
        lax.fori_loop(0, rows, fill, 0)

    def plane_of(e):
        return e + (1 - half) * (top - 2 * e)

    for e in range(own + 2, both):
        line(1, plane_of(e), 1, rows)
    for turn, q in enumerate(order):
        swaps[turn].wait_recv()
        plane = q + (1 - half) * (own - 1 - 2 * q)
        if turn == 0:
            @pl.when(half == 0)
            def _():
                remote(
                    swap.at[0, pl.ds(0, rows)], zland.at[0, 0], z_send.at[0, 1], z_recv.at[0, 0], upper
                ).start()

            @pl.when(half == 1)
            def _():
                remote(
                    swap.at[0, pl.ds(1, rows)], zland.at[0, 1], z_send.at[0, 0], z_recv.at[0, 1], lower
                ).start()

        def fill(r, _):
            field[0, 1 + own * (1 - half) + plane, shift + r, inner, :] = swap[turn, r].astype(
                jnp.float32
            )
            return 0

        lax.fori_loop(0, rows + 1, fill, 0)
        if turn >= 1:
            line(1, plane_of(q + 2), 1, rows)
    line(1, plane_of(2), 1, rows)
    fill_z(0, 0, 0)
    line(1, 1, 1, rows)
    fill_z(0, 0, 1)
    line(1, both, 1, rows)

    edge = rows - (rows - 1) * half
    started = []

    def send_edges(sweep):
        held = early.at[sweep - 1] if sweep < SWEEPS else state_ref
        copies = [
            remote(held.at[0], zland.at[sweep, 1], z_send.at[sweep, 0], z_recv.at[sweep, 1], lower),
        ]
        if sweep < SWEEPS:
            copies.append(remote(
                held.at[both - 1], zland.at[sweep, 0], z_send.at[sweep, 1], z_recv.at[sweep, 0], upper
            ))
        ycopy = remote(
            held.at[pl.ds(0, both), edge - 1], yland.at[sweep - 1], y_send.at[sweep - 1],
            y_recv.at[sweep - 1], partner,
        )
        if sweep < SWEEPS:
            copies.append(ycopy)
        for copy in copies:
            copy.start()
        started.extend(copies)
        return ycopy

    def fill_y(buf, sweep, ycopy):
        ycopy.wait_recv()

        def fill(p, _):
            field[buf, p + 1, (rows + 1) * (1 - half), inner, :] = yland[sweep - 1, p].astype(jnp.float32)
            return 0
        lax.fori_loop(0, both, fill, 0)

    for sweep in range(2, SWEEPS + 1):
        ycopy = send_edges(sweep - 1)
        src = (sweep + 1) % 2

        def middle(i, _):
            line(sweep, i + 2, 1 + half, rows - 1)
            return 0
        lax.fori_loop(0, both - 2, middle, 0)
        fill_y(src, sweep - 1, ycopy)

        def border(i, _):
            row(sweep, i + 2, edge)
            return 0
        lax.fori_loop(0, both - 2, border, 0)
        fill_z(src, sweep - 1, 0)
        line(sweep, 1, 1, rows)
        fill_z(src, sweep - 1, 1)
        line(sweep, both, 1, rows)

    ycopy = send_edges(SWEEPS)

    @pl.when(half == 1)
    def _():
        ycopy.start()

    last = SWEEPS % 2

    def stiff_row(p, y, place):
        here = field[last, p, y, inner, :]
        ahead = coef[1, p - 1, y - 1] * field[last, p + 1, y, inner, :]
        ahead += coef[3, p - 1, y - 1] * field[last, p, y + 1, inner, :]
        ahead += coef[5, p - 1, y - 1] * field[last, p, y, pl.ds(base + 1, depth), :]
        value = coef[6, p - 1, y - 1] * (here - 2.0 * ahead)
        high = value.astype(jnp.bfloat16)
        rest = (value - high.astype(jnp.float32)).astype(jnp.bfloat16)
        rhs[place, :, pl.ds(0, width)] = (here * coef[7, p - 1, y - 1]).astype(jnp.bfloat16)
        rhs[place, :, pl.ds(width, width)] = high
        rhs[place, :, pl.ds(2 * width, width)] = rest

    def gram(left, count):
        right = rhs[pl.ds(0, count)].reshape(count * depth, 3 * width)
        part = lax.dot_general(
            left.reshape(count * depth, width), right, (((0,), (0,)), ((), ())),
            preferred_element_type=jnp.float32,
        )
        gram_ref[pl.ds(0, width), :] += part[:, :width]
        gram_ref[pl.ds(width, width), :] += part[:, width:2 * width] + part[:, 2 * width:]

    gram_ref[...] = jnp.zeros_like(gram_ref)

    def inside(i, _):
        def body(y, _):
            stiff_row(i + 1, y + 1, y)
            return 0
        lax.fori_loop(0, rows - 1, body, 0)
        gram(state_ref[i, pl.ds(0, rows - 1)], rows - 1)
        return 0
    lax.fori_loop(0, both - 1, inside, 0)

    @pl.when(half == 0)
    def _():
        fill_y(last, SWEEPS, ycopy)

    @pl.when(half == 1)
    def _():
        def clear(p, _):
            field[last, p + 1, rows + 1, inner, :] = jnp.zeros((depth, width), jnp.float32)
            return 0
        lax.fori_loop(0, both, clear, 0)

    def side(i, _):
        stiff_row(i + 1, rows, i)
        return 0
    lax.fori_loop(0, both - 1, side, 0)
    gram(state_ref[pl.ds(0, both - 1), rows - 1], both - 1)
    fill_z(last, SWEEPS, 1)

    def roof(y, _):
        stiff_row(both, y + 1, y)
        return 0
    lax.fori_loop(0, rows, roof, 0)
    gram(state_ref[both - 1], rows)

    class_copies[0].wait_send()
    for place in range(2):
        remote(
            class_ref.at[0], class_low, class_send.at[1 + place], class_recv.at[1], partner
        ).wait_send()
    for copy in swaps:
        copy.wait_send()
    for direction in range(2):
        remote(
            snap_ref.at[0, pl.ds(0, rows)], zland.at[0, 0], z_send.at[0, direction], z_recv.at[0, 0], lower
        ).wait_send()
    for copy in started:
        copy.wait_send()

    @pl.when(half == 1)
    def _():
        ycopy.wait_send()


def relax_and_gram(snap, classes, yface, zface, face, members):
    own, rows_all, depth, width = snap.shape
    both, rows = 2 * own, rows_all // 2
    vmem = pl.BlockSpec(memory_space=pltpu.VMEM)
    f32, bf16 = jnp.float32, jnp.bfloat16
    dma = pltpu.SemaphoreType.DMA
    return pl.pallas_call(
        functools.partial(relax_kernel, members=members),
        out_shape=(
            jax.ShapeDtypeStruct((both, rows, depth, width), bf16),
            jax.ShapeDtypeStruct((2 * width, width), f32),
        ),
        in_specs=[vmem] * 5,
        out_specs=(vmem, vmem),
        scratch_shapes=[
            pltpu.VMEM((2, both + 2, rows + 2, depth + 16, width), f32),
            pltpu.VMEM((8, both, rows, depth, width), f32),
            pltpu.VMEM((8, rows_all, depth), f32),
            pltpu.VMEM((both + 2, rows_all, depth), f32),
            pltpu.VMEM((2, rows_all, width), f32),
            pltpu.VMEM((SWEEPS - 1, both, rows, depth, width), bf16),
            pltpu.VMEM((own, rows + 1, depth, width), bf16),
            pltpu.VMEM((SWEEPS + 1, 2, rows, depth, width), bf16),
            pltpu.VMEM((SWEEPS, both, depth, width), bf16),
            pltpu.VMEM((max(both, rows), depth, 3 * width), bf16),
            pltpu.VMEM((own, rows_all, depth), jnp.int32),
            pltpu.VMEM((rows_all, depth), jnp.int32),
            pltpu.VMEM((rows_all, depth), jnp.int32),
            dma((own,)),
            dma((own,)),
            dma((SWEEPS + 1, 2)),
            dma((SWEEPS + 1, 2)),
            dma((SWEEPS,)),
            dma((SWEEPS,)),
            dma((3,)),
            dma((3,)),
        ],
        compiler_params=pltpu.CompilerParams(
            collective_id=0, has_side_effects=True, vmem_limit_bytes=60 << 20
        ),
    )(snap, classes, yface, zface, face)


def eliminate_spd(full, size, block):
    lanes = lax.broadcasted_iota(jnp.int32, (block, size), 1)
    rows = lax.broadcasted_iota(jnp.int32, (block, size), 0)
    wide = lax.broadcasted_iota(jnp.int32, (size, size), 1)
    for first in range(0, size, block):
        panel = full[first:first + block]
        signed = jnp.where(lanes < first, -panel, panel) if first else panel
        for i in range(block):
            col = first + i
            column = panel[:, col:col + 1]
            pivot = 1.0 / panel[i:i + 1, col:col + 1]
            row = jnp.where(lanes[:1] == col, 1.0, panel[i:i + 1]) * pivot
            cleared = jnp.where(lanes == col, 0.0, panel)
            panel = jnp.where(rows == i, row, cleared - column * row)
        inside = (wide >= first) & (wide < first + block)
        update = lax.dot_general(
            signed, panel, (((0,), (0,)), ((), ())),
            precision=lax.Precision.HIGHEST, preferred_element_type=jnp.float32,
        )
        rest = jnp.where(inside, 0.0, full) - update
        parts = []
        if first:
            parts.append(rest[:first])
        parts.append(panel)
        if first + block < size:
            parts.append(rest[first + block:])
        full = jnp.concatenate(parts, axis=0)
    return full


def normalize(inner, vectors):
    count = inner.shape[0]
    rows = lax.broadcasted_iota(jnp.int32, (count, 1), 0)
    eye = lax.broadcasted_iota(jnp.int32, (count, count), 0) == lax.broadcasted_iota(
        jnp.int32, (count, count), 1
    )
    for i in range(count - 1):
        factor = inner[:, i:i + 1] * (1.0 / inner[i:i + 1, i:i + 1])
        factor = jnp.where(rows > i, factor, 0.0)
        lead, mate = inner[i:i + 1], vectors[i:i + 1]
        inner = inner - factor * lead
        vectors = vectors - factor * mate
    diagonal = jnp.sum(jnp.where(eye, inner, 0.0), axis=1, keepdims=True)
    return vectors / jnp.sqrt(diagonal)


def modes_kernel(
    snaps_ref, gram_ref, start_ref, corr_ref, out_ref,
    slots, summed, total, stage, send_sem, recv_sem, send_two, recv_two, send_out, recv_out,
    *, members, owners, own, cell_count,
):
    me_sub = lax.axis_index("sub")
    me_nbhd = lax.axis_index("nbhd")
    size = gram_ref.shape[1]
    chunk = 2 * size // members

    def sub_at(step):
        return lax.rem(me_sub + step, members)

    half = lax.rem(me_sub, 2)
    tower = me_sub - half
    planes = own
    across = owners // planes
    mine = across // 2
    from_half = lax.rem(me_nbhd, across) // mine
    whole = jnp.where(from_half == half, 1, 0)

    barrier = pltpu.get_barrier_semaphore()
    for step in range(1, members):
        pl.semaphore_signal(barrier, inc=1, device_id=(me_nbhd, sub_at(step)), device_id_type=MESH)

    def is_me(nbhd):
        return jnp.logical_and(nbhd == me_nbhd, from_half == half)

    for nbhd in range(owners):
        @pl.when(jnp.logical_not(is_me(nbhd)))
        def _():
            pl.semaphore_signal(
                barrier, inc=1, device_id=(nbhd, tower + from_half), device_id_type=MESH
            )
    pl.semaphore_wait(barrier, members - 1 + owners - whole)

    def part(owner):
        return pl.ds(pl.multiple_of(owner * chunk, chunk), chunk)

    copies = []
    for step in range(1, members):
        peer = sub_at(step)
        copy = pltpu.make_async_remote_copy(
            src_ref=gram_ref.at[part(peer)],
            dst_ref=slots.at[step],
            send_sem=send_sem.at[step],
            recv_sem=recv_sem.at[step],
            device_id=(me_nbhd, peer),
            device_id_type=MESH,
        )
        copy.start()
        copies.append(copy)
    acc = gram_ref[part(me_sub)]
    for step in range(1, members):
        copies[step - 1].wait_recv()
        acc = acc + slots[step]
    summed[...] = acc
    total[part(me_sub)] = acc
    spread = []
    for step in range(1, members):
        copy = pltpu.make_async_remote_copy(
            src_ref=summed,
            dst_ref=total.at[part(me_sub)],
            send_sem=send_two.at[step],
            recv_sem=recv_two.at[step],
            device_id=(me_nbhd, sub_at(step)),
            device_id_type=MESH,
        )
        copy.start()
        spread.append(copy)
    for copy in spread:
        copy.wait_recv()

    dot = functools.partial(
        lax.dot_general, precision=lax.Precision.HIGHEST, preferred_element_type=jnp.float32
    )
    mass = total[:size] / cell_count
    stiff = total[size:]
    stiff = (stiff + stiff.T) * (0.5 / cell_count)
    inverse = eliminate_spd(stiff, size, 32)
    step_map = dot(mass, inverse, (((1,), (0,)), ((), ())))
    both = jnp.concatenate([step_map, dot(step_map, mass, (((1,), (0,)), ((), ())))], axis=1)
    rows = None
    for turn in range(ITERS):
        if turn == 0:
            pair = dot(start_ref[...], both, (((0,), (0,)), ((), ())))
        else:
            pair = dot(rows, both, (((1,), (0,)), ((), ())))
        solved, image = pair[:, :size], pair[:, size:]
        inner = dot(solved, image, (((1,), (1,)), ((), ())))
        inner = 0.5 * (inner + inner.T)
        rows = normalize(inner, solved)
    modes = rows.astype(jnp.bfloat16)

    def piece(index, owner):
        values = lax.dot_general(
            modes, snaps_ref[index], (((1,), (1,)), ((), ())), preferred_element_type=jnp.float32
        )
        return (values * corr_ref[me_nbhd, owner].astype(jnp.float32)).astype(jnp.bfloat16)

    def leave(step, owner, sub):
        return pltpu.make_async_remote_copy(
            src_ref=stage.at[step],
            dst_ref=out_ref.at[me_nbhd],
            send_sem=send_out.at[step],
            recv_sem=recv_out.at[me_nbhd],
            device_id=(owner, sub),
            device_id_type=MESH,
        )

    leaving = []
    for step in range(owners):
        index = lax.rem(step + me_nbhd, owners)
        level = index // mine
        owner = across * lax.rem(level, planes) + mine * half + lax.rem(index, mine)
        sub = tower + level // planes
        here = jnp.logical_and(owner == me_nbhd, sub == me_sub)
        stage[step] = piece(index, owner)

        @pl.when(jnp.logical_not(here))
        def _():
            leave(step, owner, sub).start()

        @pl.when(here)
        def _():
            out_ref[me_nbhd] = stage[step]

        leaving.append((step, owner, sub, here))
    for nbhd in range(owners):
        @pl.when(jnp.logical_not(is_me(nbhd)))
        def _():
            pltpu.make_async_remote_copy(
                src_ref=stage.at[0], dst_ref=out_ref.at[nbhd], send_sem=send_out.at[0],
                recv_sem=recv_out.at[nbhd], device_id=(nbhd, me_sub), device_id_type=MESH,
            ).wait_recv()
    for step, owner, sub, here in leaving:
        @pl.when(jnp.logical_not(here))
        def _():
            leave(step, owner, sub).wait_send()
    for copy in copies + spread:
        copy.wait_send()


def modes_and_pieces(snaps, gram, start, corr, members, owners, own, cell_count):
    pieces, cells, size = snaps.shape
    modes = start.shape[1]
    vmem = pl.BlockSpec(memory_space=pltpu.VMEM)
    return pl.pallas_call(
        functools.partial(
            modes_kernel, members=members, owners=owners, own=own, cell_count=cell_count
        ),
        out_shape=jax.ShapeDtypeStruct((owners, modes, cells), jnp.bfloat16),
        in_specs=[vmem, vmem, vmem, pl.BlockSpec(memory_space=pltpu.SMEM)],
        out_specs=vmem,
        scratch_shapes=[
            pltpu.VMEM((members, 2 * size // members, size), jnp.float32),
            pltpu.VMEM((2 * size // members, size), jnp.float32),
            pltpu.VMEM((2 * size, size), jnp.float32),
            pltpu.VMEM((owners, modes, cells), jnp.bfloat16),
            pltpu.SemaphoreType.DMA((members,)),
            pltpu.SemaphoreType.DMA((members,)),
            pltpu.SemaphoreType.DMA((members,)),
            pltpu.SemaphoreType.DMA((members,)),
            pltpu.SemaphoreType.DMA((owners,)),
            pltpu.SemaphoreType.DMA((owners,)),
        ],
        compiler_params=pltpu.CompilerParams(
            collective_id=1, has_side_effects=True, vmem_limit_bytes=32 << 20
        ),
    )(snaps, gram, start, corr)


def on_device(snap_init, channel_map, yface_vals, zface_vals, face_of, start_block, correlation):
    own, rows, depth, width = snap_init.shape[1:]
    members, owners = lax.axis_size("sub"), lax.axis_size("nbhd")
    state, gram = relax_and_gram(
        snap_init[0], channel_map[0], yface_vals[0], zface_vals[0], face_of, members
    )
    cells = own * rows * depth
    result = modes_and_pieces(
        state.reshape(owners, cells // owners, width), gram, start_block[0], correlation,
        members, owners, own, float(cells * members),
    )
    return result[None, None]


def solution(mesh):
    return jax.shard_map(
        on_device,
        mesh=mesh,
        in_specs=(
            P("nbhd", "sub", None, None, None),
            P("nbhd", "sub", None, None),
            P("nbhd", None, None),
            P("nbhd", None, None),
            P("nbhd", None),
            P("nbhd", None, None),
            P(),
        ),
        out_specs=P("nbhd", "sub", None, None, None),
        check_vma=False,
    )
```

time: 202 us -> 112 us (0.55)
  waiting for transfers between devices: 49.8 us -> 0 us
  Pallas kernels: 66.5 us -> 108 us
  starting transfers between devices: 35.2 us -> 0 us
  other arithmetic: 25.6 us -> 0 us
  local copies, waits for them, and re-layouts: 15.4 us -> 3.88 us
  matrix products: 8.96 us -> 0 us
    pallas_call x0 -> x1, Pallas kernels: none -> 52.6 us  [relax_and_gram(): pl.pallas_call(functools.partial(relax_kernel, members=members), out_shap...]
    ppermute x10 -> x0, waiting for transfers between devices: 49.8 us -> none  [the longest x5 33 us: with_halo(): lax.ppermute(head, axis, [((i + 1) % count, i) for i in range(ends)])]
    ppermute x10 -> x0, starting transfers between devices: 35.2 us -> none  [the longest x5 28.6 us: with_halo(): lax.ppermute(tail, axis, [(i, (i + 1) % count) for i in range(ends)])]
    convert_element_type x4 -> x0, other arithmetic: 25.3 us -> none  [the longest x3 23.4 us: relax(): jnp.where(inside[:, None, None, None], updated, jnp.float32(0.0))]
    slice x16 -> x0, local copies, waits for them, and re-layouts: 14.5 us -> none  [the longest x4 5.93 us: face_terms(): middle[:, :, :-1]]
    pallas_call x1, Pallas kernels: 66.5 us -> 55 us  [modes_and_pieces(): pl.pallas_call(functools.partial(modes_kernel, members=members, owners=ow...]
    dot_general x2 -> x0, matrix products: 8.96 us -> none  [the longest x1 7.5 us: gram_terms(): lax.dot_general(flat, stiff_flat, dims, preferred_element_type=jnp.float32)]
    unnamed x14 -> x8, local copies, waits for them, and re-layouts: 0.87 us -> 3.88 us
  transfers between devices with their start and end apart: 10 -> 0, of which waited for: 7 -> 0; matrix products, arithmetic and copies ran while one was open for 7% -> 0% of each run, Pallas kernels for 0% -> 0%
where the time goes in v2:
time: 112 us
  Pallas kernels  108 us (96%)
  local copies, waits for them, and re-layouts  3.88 us (3%)
    pallas_call x1, Pallas kernels, modes_and_pieces(): pl.pallas_call(functools.partial(modes_kernel, members=members, owners=ow...  55 us
    pallas_call x1, Pallas kernels, relax_and_gram(): pl.pallas_call(functools.partial(relax_kernel, members=members), out_shap...  52.6 us
    unnamed x8, local copies, waits for them, and re-layouts  3.88 us

profile of v2, /device:TPU:1, one launch (start us, length us, event | category | flops | bytes accessed | tf_op | source)
XLA Modules:
  0.0 111.6 jit_solution(9363228189779215380)
XLA Ops:
  0.0 0.0 copy-start.2
  0.0 0.8 copy.8
  0.8 52.6 %shard_map.73 = (bf16[8,8,96,128]{3,2,1,0:T(8,128)(2,1)}, f32[256,128]{1,0:T(8,128)}) custom-call(bf16[4,16,96,128]{3,2,1,0:T(8,128)(2,1)} %bitcast.10, s32[4,16,96]{2,1,0:T(8,128)} %bitcast.11, bf16[96,128]{1,0:T(8,128)(2,1)} %bitcast.12, bf16[16,128]{1,0:T(8,128)(2,1)} %bitcast.13, s32[1,128]{1,0:T(1,128)} %face_ref.1), custom_call_target="tpu_custom_call" | custom-call | tf_op jit(solution)/shard_map/pallas_call | solution.py:400
  53.5 0.0 copy-done.2
  53.5 0.0 copy-start
  53.5 1.4 %copy-done = bf16[8,8,96,128]{3,2,1,0:T(8,128)(2,1)S(1)} copy-done((bf16[8,8,96,128]{3,2,1,0:T(8,128)(2,1)S(1)}, bf16[8,8,96,128]{3,2,1,0:T(8,128)(2,1)}, u32[]{:S(2)}) %copy-start) | copy-done | bytes 1572888
  54.9 0.0 copy-start.1
  54.9 0.9 copy-done.1
  55.8 55.0 %shard_map.74 = bf16[16,32,384]{2,1,0:T(8,128)(2,1)S(1)} custom-call(bf16[16,384,128]{2,1,0:T(8,128)(2,1)S(1)} %bitcast.7, f32[256,128]{1,0:T(8,128)S(1)} %copy-done.1, f32[128,32]{1,0:T(8,128)S(1)} %bitcast.9, s32[16,16]{1,0:T(8,128)S(1)} %copy-done.2), custom_call_target="tpu_custom_call" | custom-call | tf_op jit(solution)/shard_map/pallas_call | solution.py:630
  110.8 0.7 copy.10
Async XLA Ops:
  0.0 53.5 %copy-start.2 = (s32[16,16]{1,0:T(8,128)S(1)}, s32[16,16]{1,0:T(8,128)}, u32[]{:S(2)}) copy-start(s32[16,16]{1,0:T(8,128)} %corr_ref.1) | copy-start | bytes 3076
  53.5 1.4 %copy-start = (bf16[8,8,96,128]{3,2,1,0:T(8,128)(2,1)S(1)}, bf16[8,8,96,128]{3,2,1,0:T(8,128)(2,1)}, u32[]{:S(2)}) copy-start(bf16[8,8,96,128]{3,2,1,0:T(8,128)(2,1)} %get-tuple-element.7) | copy-start | bytes 4718596
  54.9 0.9 copy-start.1

commit v3 on v2

--- a/solution.py
+++ b/solution.py
@@ -434,20 +434,39 @@
     )(snap, classes, yface, zface, face)
 
 
+TILE = 8
+
+
+def spread(tile, col, width):
+    return jnp.broadcast_to(tile[:, col:col + 1], (tile.shape[0], width))
+
+
 def eliminate_spd(full, size, block):
-    lanes = lax.broadcasted_iota(jnp.int32, (block, size), 1)
-    rows = lax.broadcasted_iota(jnp.int32, (block, size), 0)
+    lanes = lax.broadcasted_iota(jnp.int32, (TILE, size), 1)
+    rows = lax.broadcasted_iota(jnp.int32, (TILE, size), 0)
     wide = lax.broadcasted_iota(jnp.int32, (size, size), 1)
+    block_lanes = lax.broadcasted_iota(jnp.int32, (block, size), 1)
+    count = block // TILE
     for first in range(0, size, block):
         panel = full[first:first + block]
-        signed = jnp.where(lanes < first, -panel, panel) if first else panel
-        for i in range(block):
-            col = first + i
-            column = panel[:, col:col + 1]
-            pivot = 1.0 / panel[i:i + 1, col:col + 1]
-            row = jnp.where(lanes[:1] == col, 1.0, panel[i:i + 1]) * pivot
-            cleared = jnp.where(lanes == col, 0.0, panel)
-            panel = jnp.where(rows == i, row, cleared - column * row)
+        signed = jnp.where(block_lanes < first, -panel, panel) if first else panel
+        tiles = [panel[TILE * u:TILE * (u + 1)] for u in range(count)]
+        for t in range(count):
+            base = first + TILE * t
+            columns = [[spread(tile, base + j, size) for tile in tiles] for j in range(TILE)]
+            for i in range(TILE):
+                here = rows == i
+                at_col = lanes == base + i
+                lead = columns[i]
+                pivot = 1.0 / lead[t][i:i + 1]
+                row = jnp.where(at_col[:1], 1.0, tiles[t][i:i + 1]) * pivot
+                for j in range(i + 1, TILE):
+                    scaled = columns[j][t][i:i + 1] * pivot
+                    columns[j] = [columns[j][u] - lead[u] * scaled for u in range(count)]
+                    columns[j][t] = jnp.where(here, scaled, columns[j][t])
+                tiles = [jnp.where(at_col, 0.0, tiles[u]) - lead[u] * row for u in range(count)]
+                tiles[t] = jnp.where(here, row, tiles[t])
+        panel = jnp.concatenate(tiles, axis=0)
         inside = (wide >= first) & (wide < first + block)
         update = lax.dot_general(
             signed, panel, (((0,), (0,)), ((), ())),
@@ -465,19 +484,35 @@
 
 
 def normalize(inner, vectors):
-    count = inner.shape[0]
-    rows = lax.broadcasted_iota(jnp.int32, (count, 1), 0)
-    eye = lax.broadcasted_iota(jnp.int32, (count, count), 0) == lax.broadcasted_iota(
-        jnp.int32, (count, count), 1
-    )
-    for i in range(count - 1):
-        factor = inner[:, i:i + 1] * (1.0 / inner[i:i + 1, i:i + 1])
-        factor = jnp.where(rows > i, factor, 0.0)
-        lead, mate = inner[i:i + 1], vectors[i:i + 1]
-        inner = inner - factor * lead
-        vectors = vectors - factor * mate
-    diagonal = jnp.sum(jnp.where(eye, inner, 0.0), axis=1, keepdims=True)
-    return vectors / jnp.sqrt(diagonal)
+    width = vectors.shape[1]
+    count = inner.shape[0] // TILE
+    rows = lax.broadcasted_iota(jnp.int32, (TILE, width), 0)
+    left = [inner[TILE * u:TILE * (u + 1)] for u in range(count)]
+    right = [vectors[TILE * u:TILE * (u + 1)] for u in range(count)]
+    scales = []
+    for t in range(count):
+        columns = [
+            [spread(left[u], TILE * t + j, width) for u in range(t, count)] for j in range(TILE)
+        ]
+        scale = jnp.zeros((TILE, width), jnp.float32)
+        for i in range(TILE):
+            lead = columns[i]
+            value = lead[0][i:i + 1]
+            pivot = 1.0 / value
+            scale = jnp.where(rows == i, value, scale)
+            for j in range(i + 1, TILE):
+                scaled = columns[j][0][i:i + 1] * pivot
+                columns[j] = [column - part * scaled for column, part in zip(columns[j], lead)]
+            below = [jnp.where(rows > i, lead[0], 0.0)] + lead[1:]
+            mate = right[t][i:i + 1] * pivot
+            for u in range(t, count):
+                right[u] = right[u] - below[u - t] * mate
+            if t + 1 < count:
+                ahead = left[t][i:i + 1] * pivot[:, :left[t].shape[1]]
+                for u in range(t, count):
+                    left[u] = left[u] - below[u - t][:, :left[t].shape[1]] * ahead
+        scales.append(scale)
+    return jnp.concatenate([tile / jnp.sqrt(scale) for tile, scale in zip(right, scales)], axis=0)
 
 
 def modes_kernel(

time: 112 us -> 97 us (0.87)
  Pallas kernels: 108 us -> 92.3 us
    pallas_call x1, Pallas kernels: 55 us -> 39.6 us  [modes_and_pieces(): pl.pallas_call(functools.partial(modes_kernel, members=members, owners=ow...]
where the time goes in v3:
time: 97 us; the launch traced here: 96.2 us
  Pallas kernels  92.3 us (95%)
  local copies, waits for them, and re-layouts  3.88 us (4%)
    pallas_call x1, Pallas kernels, relax_and_gram(): pl.pallas_call(functools.partial(relax_kernel, members=members), out_shap...  52.6 us
    pallas_call x1, Pallas kernels, modes_and_pieces(): pl.pallas_call(functools.partial(modes_kernel, members=members, owners=ow...  39.6 us
    unnamed x8, local copies, waits for them, and re-layouts  3.88 us

profile of v3, /device:TPU:1, one launch (start us, length us, event | category | flops | bytes accessed | tf_op | source)
XLA Modules:
  0.0 96.2 jit_solution(7647129398706645194)
XLA Ops:
  0.0 0.0 copy-start.2
  0.0 0.8 copy.8
  0.8 52.6 %shard_map.73 = (bf16[8,8,96,128]{3,2,1,0:T(8,128)(2,1)}, f32[256,128]{1,0:T(8,128)}) custom-call(bf16[4,16,96,128]{3,2,1,0:T(8,128)(2,1)} %bitcast.10, s32[4,16,96]{2,1,0:T(8,128)} %bitcast.11, bf16[96,128]{1,0:T(8,128)(2,1)} %bitcast.12, bf16[16,128]{1,0:T(8,128)(2,1)} %bitcast.13, s32[1,128]{1,0:T(1,128)} %face_ref.1), custom_call_target="tpu_custom_call" | custom-call | tf_op jit(solution)/shard_map/pallas_call | solution.py:400
  53.5 0.0 copy-done.2
  53.5 0.0 copy-start
  53.5 1.4 %copy-done = bf16[8,8,96,128]{3,2,1,0:T(8,128)(2,1)S(1)} copy-done((bf16[8,8,96,128]{3,2,1,0:T(8,128)(2,1)S(1)}, bf16[8,8,96,128]{3,2,1,0:T(8,128)(2,1)}, u32[]{:S(2)}) %copy-start) | copy-done | bytes 1572888
  54.9 0.0 copy-start.1
  54.9 0.9 copy-done.1
  55.8 39.6 %shard_map.74 = bf16[16,32,384]{2,1,0:T(8,128)(2,1)S(1)} custom-call(bf16[16,384,128]{2,1,0:T(8,128)(2,1)S(1)} %bitcast.7, f32[256,128]{1,0:T(8,128)S(1)} %copy-done.1, f32[128,32]{1,0:T(8,128)S(1)} %bitcast.9, s32[16,16]{1,0:T(8,128)S(1)} %copy-done.2), custom_call_target="tpu_custom_call" | custom-call | tf_op jit(solution)/shard_map/pallas_call | solution.py:665
  95.4 0.7 copy.10
Async XLA Ops:
  0.0 53.5 %copy-start.2 = (s32[16,16]{1,0:T(8,128)S(1)}, s32[16,16]{1,0:T(8,128)}, u32[]{:S(2)}) copy-start(s32[16,16]{1,0:T(8,128)} %corr_ref.1) | copy-start | bytes 3076
  53.5 1.4 %copy-start = (bf16[8,8,96,128]{3,2,1,0:T(8,128)(2,1)S(1)}, bf16[8,8,96,128]{3,2,1,0:T(8,128)(2,1)}, u32[]{:S(2)}) copy-start(bf16[8,8,96,128]{3,2,1,0:T(8,128)(2,1)} %get-tuple-element.7) | copy-start | bytes 4718596
  54.9 0.9 copy-start.1

commit v4 on v3

--- a/solution.py
+++ b/solution.py
@@ -79,7 +79,7 @@
         for copy in class_sends(own - 1, class_low, 1, (upper, cross)):
             copy.start()
 
-    order = [0] + list(range(own - 1, 0, -1))
+    order = [0, 1] + list(range(own - 1, 1, -1))
     swaps = []
     for turn, q in enumerate(order):
         plane = q + half * (own - 1 - 2 * q)
@@ -93,14 +93,15 @@
     @pl.when(half == 0)
     def _():
         remote(
-            snap_ref.at[0, pl.ds(0, rows)], zland.at[0, 1], z_send.at[0, 0], z_recv.at[0, 1], lower
+            snap_ref.at[0, pl.ds(0, rows)], zland.at[0, 1], z_send.at[0, 0, 0],
+            z_recv.at[0, 1, 0], lower
         ).start()
 
     @pl.when(half == 1)
     def _():
         remote(
-            snap_ref.at[own - 1, pl.ds(rows, rows)], zland.at[0, 0], z_send.at[0, 1],
-            z_recv.at[0, 0], upper
+            snap_ref.at[own - 1, pl.ds(rows, rows)], zland.at[0, 0], z_send.at[0, 1, 0],
+            z_recv.at[0, 0, 0], upper
         ).start()
 
     shift = 1 - half
@@ -211,16 +212,59 @@
             return 0
         lax.fori_loop(0, count, body, 0)
 
-    def fill_z(buf, round_no, side):
-        remote(
-            zland.at[round_no, side], zland.at[round_no, side], z_send.at[round_no, side],
-            z_recv.at[round_no, side], lower,
+    chunk = rows // 2
+    edge = rows - (rows - 1) * half
+
+    def chunk_at(part):
+        return chunk * half if part == 0 else chunk - chunk * half
+
+    def held(sweep):
+        return early.at[sweep - 1] if sweep < SWEEPS else state_ref
+
+    def send_z(sweep, side, part):
+        cells = pl.ds(chunk_at(part), chunk)
+        remote(
+            held(sweep).at[side * (both - 1), cells], zland.at[sweep, 1 - side, cells],
+            z_send.at[sweep, side, part], z_recv.at[sweep, 1 - side, part], at(me - 2 + 4 * side),
+        ).start()
+
+    def send_y(sweep, part, first, count):
+        planes = pl.ds(first, count)
+        remote(
+            held(sweep).at[planes, edge - 1], yland.at[sweep - 1, planes], y_send.at[sweep - 1, part],
+            y_recv.at[sweep - 1, part], partner,
+        ).start()
+
+    def take_z(buf, sweep, side, part):
+        cells = pl.ds(0, rows if sweep == 0 else chunk)
+        remote(
+            zland.at[sweep, side, cells], zland.at[sweep, side, cells], z_send.at[sweep, side, part],
+            z_recv.at[sweep, side, part], lower,
         ).wait_recv()
-
-        def fill(y, _):
-            field[buf, top * side, y + 1, inner, :] = zland[round_no, side, y].astype(jnp.float32)
-            return 0
-        lax.fori_loop(0, rows, fill, 0)
+        first = 0 if sweep == 0 else chunk_at(part)
+
+        def fill(i, _):
+            field[buf, top * side, first + i + 1, inner, :] = zland[sweep, side, first + i].astype(
+                jnp.float32
+            )
+            return 0
+        lax.fori_loop(0, rows if sweep == 0 else chunk, fill, 0)
+
+    y_parts = ((1, own - 1), (own, own - 1), (0, 1), (both - 1, 1))
+
+    def take_y(buf, sweep, part):
+        first, count = y_parts[part]
+        planes = pl.ds(first, count)
+        remote(
+            yland.at[sweep - 1, planes], yland.at[sweep - 1, planes], y_send.at[sweep - 1, part],
+            y_recv.at[sweep - 1, part], partner,
+        ).wait_recv()
+
+        def fill(i, _):
+            p = first + i
+            field[buf, p + 1, (rows + 1) * (1 - half), inner, :] = yland[sweep - 1, p].astype(jnp.float32)
+            return 0
+        lax.fori_loop(0, count, fill, 0)
 
     def plane_of(e):
         return e + (1 - half) * (top - 2 * e)
@@ -234,13 +278,15 @@
             @pl.when(half == 0)
             def _():
                 remote(
-                    swap.at[0, pl.ds(0, rows)], zland.at[0, 0], z_send.at[0, 1], z_recv.at[0, 0], upper
+                    swap.at[0, pl.ds(0, rows)], zland.at[0, 0], z_send.at[0, 1, 0], z_recv.at[0, 0, 0],
+                    upper,
                 ).start()
 
             @pl.when(half == 1)
             def _():
                 remote(
-                    swap.at[0, pl.ds(1, rows)], zland.at[0, 1], z_send.at[0, 0], z_recv.at[0, 1], lower
+                    swap.at[0, pl.ds(1, rows)], zland.at[0, 1], z_send.at[0, 0, 0], z_recv.at[0, 1, 0],
+                    lower,
                 ).start()
 
         def fill(r, _):
@@ -250,69 +296,63 @@
             return 0
 
         lax.fori_loop(0, rows + 1, fill, 0)
-        if turn >= 1:
+        if turn == 1:
+            take_z(0, 0, 0, 0)
+            take_z(0, 0, 1, 0)
+            for e, side in ((both, half), (1, 1 - half)):
+                line(1, plane_of(e), 1, rows)
+                send_z(1, side, 0)
+                send_z(1, side, 1)
+                send_y(1, 2 + side, side * (both - 1), 1)
+        if turn >= 2:
             line(1, plane_of(q + 2), 1, rows)
+        if q == own - 1:
+            send_y(1, half, 1 + (own - 1) * half, own - 1)
+    line(1, plane_of(3), 1, rows)
     line(1, plane_of(2), 1, rows)
-    fill_z(0, 0, 0)
-    line(1, 1, 1, rows)
-    fill_z(0, 0, 1)
-    line(1, both, 1, rows)
-
-    edge = rows - (rows - 1) * half
-    started = []
-
-    def send_edges(sweep):
-        held = early.at[sweep - 1] if sweep < SWEEPS else state_ref
-        copies = [
-            remote(held.at[0], zland.at[sweep, 1], z_send.at[sweep, 0], z_recv.at[sweep, 1], lower),
-        ]
+    send_y(1, 1 - half, 1 + (own - 1) * (1 - half), own - 1)
+
+    def only_if_last(sweep, action):
         if sweep < SWEEPS:
-            copies.append(remote(
-                held.at[both - 1], zland.at[sweep, 0], z_send.at[sweep, 1], z_recv.at[sweep, 0], upper
-            ))
-        ycopy = remote(
-            held.at[pl.ds(0, both), edge - 1], yland.at[sweep - 1], y_send.at[sweep - 1],
-            y_recv.at[sweep - 1], partner,
-        )
-        if sweep < SWEEPS:
-            copies.append(ycopy)
-        for copy in copies:
-            copy.start()
-        started.extend(copies)
-        return ycopy
-
-    def fill_y(buf, sweep, ycopy):
-        ycopy.wait_recv()
-
-        def fill(p, _):
-            field[buf, p + 1, (rows + 1) * (1 - half), inner, :] = yland[sweep - 1, p].astype(jnp.float32)
-            return 0
-        lax.fori_loop(0, both, fill, 0)
+            action()
+        else:
+            pl.when(half == 1)(action)
 
     for sweep in range(2, SWEEPS + 1):
-        ycopy = send_edges(sweep - 1)
         src = (sweep + 1) % 2
+        sides = (0, 1) if sweep < SWEEPS else (0,)
 
         def middle(i, _):
             line(sweep, i + 2, 1 + half, rows - 1)
             return 0
         lax.fori_loop(0, both - 2, middle, 0)
-        fill_y(src, sweep - 1, ycopy)
+        for side in (0, 1):
+            take_z(src, sweep - 1, side, 0)
+            line(sweep, 1 + side * (both - 1), 1 + chunk_at(0), chunk)
+            if side in sides:
+                send_z(sweep, side, 0)
+        take_y(src, sweep - 1, 0)
+        take_y(src, sweep - 1, 1)
 
         def border(i, _):
             row(sweep, i + 2, edge)
             return 0
         lax.fori_loop(0, both - 2, border, 0)
-        fill_z(src, sweep - 1, 0)
-        line(sweep, 1, 1, rows)
-        fill_z(src, sweep - 1, 1)
-        line(sweep, both, 1, rows)
-
-    ycopy = send_edges(SWEEPS)
-
-    @pl.when(half == 1)
-    def _():
-        ycopy.start()
+
+        def first_parts():
+            send_y(sweep, 0, *y_parts[0])
+            send_y(sweep, 1, *y_parts[1])
+        only_if_last(sweep, first_parts)
+        for side in (0, 1):
+            take_y(src, sweep - 1, 2 + side)
+            take_z(src, sweep - 1, side, 1)
+            line(sweep, 1 + side * (both - 1), 1 + chunk_at(1), chunk)
+            if side in sides:
+                send_z(sweep, side, 1)
+
+            def last_part():
+                send_y(sweep, 2 + side, *y_parts[2 + side])
+            only_if_last(sweep, last_part)
 
     last = SWEEPS % 2
 
@@ -350,7 +390,8 @@
 
     @pl.when(half == 0)
     def _():
-        fill_y(last, SWEEPS, ycopy)
+        for part in range(4):
+            take_y(last, SWEEPS, part)
 
     @pl.when(half == 1)
     def _():
@@ -364,7 +405,8 @@
         return 0
     lax.fori_loop(0, both - 1, side, 0)
     gram(state_ref[pl.ds(0, both - 1), rows - 1], both - 1)
-    fill_z(last, SWEEPS, 1)
+    take_z(last, SWEEPS, 1, 0)
+    take_z(last, SWEEPS, 1, 1)
 
     def roof(y, _):
         stiff_row(both, y + 1, y)
@@ -379,16 +421,34 @@
         ).wait_send()
     for copy in swaps:
         copy.wait_send()
-    for direction in range(2):
-        remote(
-            snap_ref.at[0, pl.ds(0, rows)], zland.at[0, 0], z_send.at[0, direction], z_recv.at[0, 0], lower
+    for side in range(2):
+        remote(
+            snap_ref.at[0, pl.ds(0, rows)], zland.at[0, 0], z_send.at[0, side, 0], z_recv.at[0, 0, 0], lower
         ).wait_send()
-    for copy in started:
-        copy.wait_send()
-
-    @pl.when(half == 1)
-    def _():
-        ycopy.wait_send()
+
+    def left_z(sweep, side, part):
+        cells = pl.ds(0, chunk)
+        remote(
+            held(sweep).at[0, cells], zland.at[sweep, 0, cells], z_send.at[sweep, side, part],
+            z_recv.at[sweep, 0, part], lower,
+        ).wait_send()
+
+    def left_y(sweep, part):
+        planes = pl.ds(*y_parts[part])
+        remote(
+            held(sweep).at[planes, 0], yland.at[sweep - 1, planes], y_send.at[sweep - 1, part],
+            y_recv.at[sweep - 1, part], partner,
+        ).wait_send()
+
+    for sweep in range(1, SWEEPS + 1):
+        for side in range(2 if sweep < SWEEPS else 1):
+            for part in range(2):
+                left_z(sweep, side, part)
+
+        def all_y():
+            for part in range(4):
+                left_y(sweep, part)
+        only_if_last(sweep, all_y)
 
 
 def relax_and_gram(snap, classes, yface, zface, face, members):
@@ -421,10 +481,10 @@
             pltpu.VMEM((rows_all, depth), jnp.int32),
             dma((own,)),
             dma((own,)),
-            dma((SWEEPS + 1, 2)),
-            dma((SWEEPS + 1, 2)),
-            dma((SWEEPS,)),
-            dma((SWEEPS,)),
+            dma((SWEEPS + 1, 2, 2)),
+            dma((SWEEPS + 1, 2, 2)),
+            dma((SWEEPS, 4)),
+            dma((SWEEPS, 4)),
             dma((3,)),
             dma((3,)),
         ],

time: 97 us -> 95.4 us (0.984)
  Pallas kernels: 92.3 us -> 89.7 us
    pallas_call x1, Pallas kernels: 52.6 us -> 50.8 us  [relax_and_gram(): pl.pallas_call(functools.partial(relax_kernel, members=members), out_shap...]
where the time goes in v4:
time: 95.4 us; the launch traced here: 93.6 us
  Pallas kernels  89.7 us (94%)
  local copies, waits for them, and re-layouts  3.88 us (4%)
    pallas_call x1, Pallas kernels, relax_and_gram(): pl.pallas_call(functools.partial(relax_kernel, members=members), out_shap...  50.8 us
    pallas_call x1, Pallas kernels, modes_and_pieces(): pl.pallas_call(functools.partial(modes_kernel, members=members, owners=ow...  38.9 us
    unnamed x8, local copies, waits for them, and re-layouts  3.88 us

profile of v4, /device:TPU:1, one launch (start us, length us, event | category | flops | bytes accessed | tf_op | source)
XLA Modules:
  0.0 93.6 jit_solution(566139587228444822)
XLA Ops:
  0.0 0.0 copy-start.2
  0.0 0.8 copy.8
  0.8 50.8 %shard_map.73 = (bf16[8,8,96,128]{3,2,1,0:T(8,128)(2,1)}, f32[256,128]{1,0:T(8,128)}) custom-call(bf16[4,16,96,128]{3,2,1,0:T(8,128)(2,1)} %bitcast.10, s32[4,16,96]{2,1,0:T(8,128)} %bitcast.11, bf16[96,128]{1,0:T(8,128)(2,1)} %bitcast.12, bf16[16,128]{1,0:T(8,128)(2,1)} %bitcast.13, s32[1,128]{1,0:T(1,128)} %face_ref.1), custom_call_target="tpu_custom_call" | custom-call | tf_op jit(solution)/shard_map/pallas_call | solution.py:460
  51.6 0.0 copy-done.2
  51.6 0.0 copy-start
  51.7 1.4 %copy-done = bf16[8,8,96,128]{3,2,1,0:T(8,128)(2,1)S(1)} copy-done((bf16[8,8,96,128]{3,2,1,0:T(8,128)(2,1)S(1)}, bf16[8,8,96,128]{3,2,1,0:T(8,128)(2,1)}, u32[]{:S(2)}) %copy-start) | copy-done | bytes 1572888
  53.1 0.0 copy-start.1
  53.1 0.9 copy-done.1
  54.0 38.9 %shard_map.74 = bf16[16,32,384]{2,1,0:T(8,128)(2,1)S(1)} custom-call(bf16[16,384,128]{2,1,0:T(8,128)(2,1)S(1)} %bitcast.7, f32[256,128]{1,0:T(8,128)S(1)} %copy-done.1, f32[128,32]{1,0:T(8,128)S(1)} %bitcast.9, s32[16,16]{1,0:T(8,128)S(1)} %copy-done.2), custom_call_target="tpu_custom_call" | custom-call | tf_op jit(solution)/shard_map/pallas_call | solution.py:725
  92.9 0.7 copy.10
Async XLA Ops:
  0.0 51.6 %copy-start.2 = (s32[16,16]{1,0:T(8,128)S(1)}, s32[16,16]{1,0:T(8,128)}, u32[]{:S(2)}) copy-start(s32[16,16]{1,0:T(8,128)} %corr_ref.1) | copy-start | bytes 3076
  51.6 1.4 %copy-start = (bf16[8,8,96,128]{3,2,1,0:T(8,128)(2,1)S(1)}, bf16[8,8,96,128]{3,2,1,0:T(8,128)(2,1)}, u32[]{:S(2)}) copy-start(bf16[8,8,96,128]{3,2,1,0:T(8,128)(2,1)} %get-tuple-element.7) | copy-start | bytes 4718596
  53.1 0.9 copy-start.1

commit v5 on v4

--- a/solution.py
+++ b/solution.py
@@ -19,7 +19,7 @@
 
 def relax_kernel(
     snap_ref, class_ref, yface_ref, zface_ref, face_ref, state_ref, gram_ref,
-    field, coef, compact, kappa, ghost_z, early, swap, zland, yland, rhs,
+    field, coef, compact, select, kappa, ghost_z, early, swap, zland, yland, rhs,
     class_pair, class_low, class_high,
     swap_send, swap_recv, z_send, z_recv, y_send, y_recv, class_send, class_recv,
     *, members,
@@ -172,22 +172,41 @@
         z_upper = jnp.concatenate([z_inner, centre[:, -1:]], axis=1)
         denom = x_lower + x_upper + y_lower + y_upper + z_lower + z_upper
         inverse = 1.0 / denom
-        compact[0] = jnp.where(has_low, face_low, 0.0) * inverse
-        compact[1] = jnp.where(has_high, face_high, 0.0) * inverse
-        compact[2] = y_lower * inverse
-        compact[3] = y_upper * inverse
-        compact[4] = z_lower * inverse
-        compact[5] = z_upper * inverse
-        compact[6] = denom
-        compact[7] = centre * (1.0 / 16.0)
-        first = pl.multiple_of(rows * half, rows)
-        for kind in range(8):
-            turned = compact[kind, pl.ds(first, rows), :].T
-            for y in range(rows):
-                coef[kind, p, y] = jnp.broadcast_to(turned[:, y:y + 1], (depth, width))
+        compact[0, p] = jnp.where(has_low, face_low, 0.0) * inverse
+        compact[1, p] = jnp.where(has_high, face_high, 0.0) * inverse
+        compact[2, p] = y_lower * inverse
+        compact[3, p] = y_upper * inverse
+        compact[4, p] = z_lower * inverse
+        compact[5, p] = z_upper * inverse
+        compact[6, p] = denom
+        compact[7, p] = centre * (1.0 / 16.0)
         return 0
 
     lax.fori_loop(0, both, coefficients, 0)
+    taken = lax.broadcasted_iota(jnp.int32, select.shape, 0)
+    given = lax.broadcasted_iota(jnp.int32, select.shape, 1)
+    select[...] = jnp.where(lax.rem(taken, rows) == given // width, 1.0, 0.0).astype(jnp.bfloat16)
+
+    def widen(kinds):
+        def one(p, _):
+            for kind in kinds:
+                exact = compact[kind, p, pl.ds(pl.multiple_of(rows * half, rows), rows), :]
+                terms = []
+                for _ in range(3):
+                    term = exact.astype(jnp.bfloat16).astype(jnp.float32)
+                    terms.append(term)
+                    exact = exact - term
+                terms.append(jnp.zeros_like(exact))
+                wide = lax.dot_general(
+                    jnp.concatenate(terms, axis=0).astype(jnp.bfloat16), select[...],
+                    (((0,), (0,)), ((), ())), preferred_element_type=jnp.float32,
+                )
+                for y in range(rows):
+                    coef[kind, p, y] = wide[:, width * y:width * (y + 1)]
+            return 0
+        lax.fori_loop(0, both, one, 0)
+
+    widen(range(6))
 
     def row(sweep, p, y):
         src, dst = (sweep + 1) % 2, sweep % 2
@@ -326,6 +345,8 @@
             line(sweep, i + 2, 1 + half, rows - 1)
             return 0
         lax.fori_loop(0, both - 2, middle, 0)
+        if sweep >= SWEEPS - 1:
+            widen((8 - 1 - SWEEPS + sweep,))
         for side in (0, 1):
             take_z(src, sweep - 1, side, 0)
             line(sweep, 1 + side * (both - 1), 1 + chunk_at(0), chunk)
@@ -468,7 +489,8 @@
         scratch_shapes=[
             pltpu.VMEM((2, both + 2, rows + 2, depth + 16, width), f32),
             pltpu.VMEM((8, both, rows, depth, width), f32),
-            pltpu.VMEM((8, rows_all, depth), f32),
+            pltpu.VMEM((8, both, rows_all, depth), f32),
+            pltpu.VMEM((4 * rows, rows * width), bf16),
             pltpu.VMEM((both + 2, rows_all, depth), f32),
             pltpu.VMEM((2, rows_all, width), f32),
             pltpu.VMEM((SWEEPS - 1, both, rows, depth, width), bf16),
@@ -657,12 +679,9 @@
     inverse = eliminate_spd(stiff, size, 32)
     step_map = dot(mass, inverse, (((1,), (0,)), ((), ())))
     both = jnp.concatenate([step_map, dot(step_map, mass, (((1,), (0,)), ((), ())))], axis=1)
-    rows = None
+    rows = start_ref[...]
     for turn in range(ITERS):
-        if turn == 0:
-            pair = dot(start_ref[...], both, (((0,), (0,)), ((), ())))
-        else:
-            pair = dot(rows, both, (((1,), (0,)), ((), ())))
+        pair = dot(rows, both, (((1,), (0,)), ((), ())))
         solved, image = pair[:, :size], pair[:, size:]
         inner = dot(solved, image, (((1,), (1,)), ((), ())))
         inner = 0.5 * (inner + inner.T)
@@ -720,7 +739,7 @@
 
 def modes_and_pieces(snaps, gram, start, corr, members, owners, own, cell_count):
     pieces, cells, size = snaps.shape
-    modes = start.shape[1]
+    modes = start.shape[0]
     vmem = pl.BlockSpec(memory_space=pltpu.VMEM)
     return pl.pallas_call(
         functools.partial(
@@ -755,7 +774,7 @@
     )
     cells = own * rows * depth
     result = modes_and_pieces(
-        state.reshape(owners, cells // owners, width), gram, start_block[0], correlation,
+        state.reshape(owners, cells // owners, width), gram, start_block[0].T, correlation,
         members, owners, own, float(cells * members),
     )
     return result[None, None]

time: 95.4 us -> 93.4 us (0.979)
    pallas_call x1, Pallas kernels: 50.8 us -> 49.7 us  [relax_and_gram(): pl.pallas_call(functools.partial(relax_kernel, members=members), out_shap...]
    unnamed x8 -> x9, local copies, waits for them, and re-layouts: 3.88 us -> 3.06 us
where the time goes in v5:
time: 93.4 us; the launch traced here: 92.5 us
  Pallas kernels  89.4 us (96%)
  local copies, waits for them, and re-layouts  3.06 us (3%)
    pallas_call x1, Pallas kernels, relax_and_gram(): pl.pallas_call(functools.partial(relax_kernel, members=members), out_shap...  49.7 us
    pallas_call x1, Pallas kernels, modes_and_pieces(): pl.pallas_call(functools.partial(modes_kernel, members=members, owners=ow...  39.7 us
    unnamed x9, local copies, waits for them, and re-layouts  3.06 us

profile of v5, /device:TPU:1, one launch (start us, length us, event | category | flops | bytes accessed | tf_op | source)
XLA Modules:
  0.0 92.5 jit_solution(3249864255343644367)
XLA Ops:
  0.0 0.0 copy-start.3
  0.0 0.0 copy-start.2
  0.0 49.7 %shard_map.73 = (bf16[8,8,96,128]{3,2,1,0:T(8,128)(2,1)}, f32[256,128]{1,0:T(8,128)}) custom-call(bf16[4,16,96,128]{3,2,1,0:T(8,128)(2,1)} %bitcast.12, s32[4,16,96]{2,1,0:T(8,128)} %bitcast.13, bf16[96,128]{1,0:T(8,128)(2,1)} %bitcast.14, bf16[16,128]{1,0:T(8,128)(2,1)} %bitcast.15, s32[1,128]{1,0:T(1,128)} %face_ref.1), custom_call_target="tpu_custom_call" | custom-call | tf_op jit(solution)/shard_map/pallas_call | solution.py:481
  49.7 0.0 copy-done.3
  49.7 0.0 copy-done.2
  49.7 0.0 copy-start
  49.7 1.4 %copy-done = bf16[8,8,96,128]{3,2,1,0:T(8,128)(2,1)S(1)} copy-done((bf16[8,8,96,128]{3,2,1,0:T(8,128)(2,1)S(1)}, bf16[8,8,96,128]{3,2,1,0:T(8,128)(2,1)}, u32[]{:S(2)}) %copy-start) | copy-done | bytes 1572888
  51.1 0.0 copy-start.1
  51.1 0.9 copy-done.1
  52.0 39.7 %shard_map.74 = bf16[16,32,384]{2,1,0:T(8,128)(2,1)S(1)} custom-call(bf16[16,384,128]{2,1,0:T(8,128)(2,1)S(1)} %bitcast.10, f32[256,128]{1,0:T(8,128)S(1)} %copy-done.1, f32[32,128]{1,0:T(8,128)S(1)} %bitcast.11, s32[16,16]{1,0:T(8,128)S(1)} %copy-done.3), custom_call_target="tpu_custom_call" | custom-call | tf_op jit(solution)/shard_map/pallas_call | solution.py:744
  91.8 0.7 copy.9
Async XLA Ops:
  0.0 49.7 %copy-start.3 = (s32[16,16]{1,0:T(8,128)S(1)}, s32[16,16]{1,0:T(8,128)}, u32[]{:S(2)}) copy-start(s32[16,16]{1,0:T(8,128)} %corr_ref.1) | copy-start | bytes 3076
  0.0 49.7 %copy-start.2 = (f32[1,128,32]{1,2,0:T(8,128)S(1)}, f32[1,128,32]{1,2,0:T(8,128)}, u32[]{:S(2)}) copy-start(f32[1,128,32]{1,2,0:T(8,128)} %param.12) | copy-start | bytes 49156
  49.7 1.4 %copy-start = (bf16[8,8,96,128]{3,2,1,0:T(8,128)(2,1)S(1)}, bf16[8,8,96,128]{3,2,1,0:T(8,128)(2,1)}, u32[]{:S(2)}) copy-start(bf16[8,8,96,128]{3,2,1,0:T(8,128)(2,1)} %get-tuple-element.7) | copy-start | bytes 4718596
  51.1 0.9 copy-start.1

commit v6 on v5

--- a/solution.py
+++ b/solution.py
@@ -17,12 +17,12 @@
     return 2.0 * left_k * right_k / (left_k + right_k)
 
 
-def relax_kernel(
-    snap_ref, class_ref, yface_ref, zface_ref, face_ref, state_ref, gram_ref,
+def relax_part(
+    snap_ref, class_ref, yface_ref, zface_ref, face_ref, state_ref, mass_ref, stiff_ref,
     field, coef, compact, select, kappa, ghost_z, early, swap, zland, yland, rhs,
-    class_pair, class_low, class_high,
+    class_pair, class_low, class_high, slab, slab_sem,
     swap_send, swap_recv, z_send, z_recv, y_send, y_recv, class_send, class_recv,
-    *, members,
+    members, mass_ready,
 ):
     me_nbhd = lax.axis_index("nbhd")
     me = lax.axis_index("sub")
@@ -50,11 +50,6 @@
             device_id=device, device_id_type=MESH,
         )
 
-    barrier = pltpu.get_barrier_semaphore()
-    for device in (partner, cross, lower, upper):
-        pl.semaphore_signal(barrier, inc=1, device_id=device, device_id_type=MESH)
-    pl.semaphore_wait(barrier, 4)
-
     class_copies = [
         remote(class_ref, class_pair, class_send.at[0], class_recv.at[0], partner),
     ]
@@ -108,12 +103,13 @@
 
     def fill_own(p, _):
         def fill(r, _):
-            field[0, 1 + own * half + p, shift + r, inner, :] = snap_ref[
+            field[0, 1 + own * half + p, shift + r, inner, :] = slab[
                 p, (rows - 1) * half + r
             ].astype(jnp.float32)
             return 0
         return lax.fori_loop(0, rows + 1, fill, 0)
 
+    pltpu.make_async_copy(snap_ref, slab, slab_sem).wait()
     lax.fori_loop(0, own, fill_own, 0)
 
     face = face_ref[...]
@@ -385,27 +381,40 @@
         value = coef[6, p - 1, y - 1] * (here - 2.0 * ahead)
         high = value.astype(jnp.bfloat16)
         rest = (value - high.astype(jnp.float32)).astype(jnp.bfloat16)
-        rhs[place, :, pl.ds(0, width)] = (here * coef[7, p - 1, y - 1]).astype(jnp.bfloat16)
-        rhs[place, :, pl.ds(width, width)] = high
-        rhs[place, :, pl.ds(2 * width, width)] = rest
-
-    def gram(left, count):
-        right = rhs[pl.ds(0, count)].reshape(count * depth, 3 * width)
-        part = lax.dot_general(
+        rhs[place, :, pl.ds(0, width)] = high
+        rhs[place, :, pl.ds(width, width)] = rest
+
+    def gram(left, count, used):
+        right = rhs[pl.ds(0, count), :, pl.ds(0, used)].reshape(count * depth, used)
+        return lax.dot_general(
             left.reshape(count * depth, width), right, (((0,), (0,)), ((), ())),
             preferred_element_type=jnp.float32,
         )
-        gram_ref[pl.ds(0, width), :] += part[:, :width]
-        gram_ref[pl.ds(width, width), :] += part[:, width:2 * width] + part[:, 2 * width:]
-
-    gram_ref[...] = jnp.zeros_like(gram_ref)
+
+    def add_stiff(left, count):
+        terms = gram(left, count, 2 * width)
+        stiff_ref[...] += terms[:, :width] + terms[:, width:]
+
+    mass_ref[...] = jnp.zeros_like(mass_ref)
+    stiff_ref[...] = jnp.zeros_like(stiff_ref)
+
+    def weigh(p, _):
+        def body(y, _):
+            here = state_ref[p, y].astype(jnp.float32)
+            rhs[y, :, pl.ds(0, width)] = (here * coef[7, p, y]).astype(jnp.bfloat16)
+            return 0
+        lax.fori_loop(0, rows, body, 0)
+        mass_ref[...] += gram(state_ref[p], rows, width)
+        return 0
+    lax.fori_loop(0, both, weigh, 0)
+    mass_ready()
 
     def inside(i, _):
         def body(y, _):
             stiff_row(i + 1, y + 1, y)
             return 0
         lax.fori_loop(0, rows - 1, body, 0)
-        gram(state_ref[i, pl.ds(0, rows - 1)], rows - 1)
+        add_stiff(state_ref[i, pl.ds(0, rows - 1)], rows - 1)
         return 0
     lax.fori_loop(0, both - 1, inside, 0)
 
@@ -425,7 +434,7 @@
         stiff_row(i + 1, rows, i)
         return 0
     lax.fori_loop(0, both - 1, side, 0)
-    gram(state_ref[pl.ds(0, both - 1), rows - 1], both - 1)
+    add_stiff(state_ref[pl.ds(0, both - 1), rows - 1], both - 1)
     take_z(last, SWEEPS, 1, 0)
     take_z(last, SWEEPS, 1, 1)
 
@@ -433,87 +442,46 @@
         stiff_row(both, y + 1, y)
         return 0
     lax.fori_loop(0, rows, roof, 0)
-    gram(state_ref[both - 1], rows)
-
-    class_copies[0].wait_send()
-    for place in range(2):
-        remote(
-            class_ref.at[0], class_low, class_send.at[1 + place], class_recv.at[1], partner
-        ).wait_send()
-    for copy in swaps:
-        copy.wait_send()
-    for side in range(2):
-        remote(
-            snap_ref.at[0, pl.ds(0, rows)], zland.at[0, 0], z_send.at[0, side, 0], z_recv.at[0, 0, 0], lower
-        ).wait_send()
-
-    def left_z(sweep, side, part):
-        cells = pl.ds(0, chunk)
-        remote(
-            held(sweep).at[0, cells], zland.at[sweep, 0, cells], z_send.at[sweep, side, part],
-            z_recv.at[sweep, 0, part], lower,
-        ).wait_send()
-
-    def left_y(sweep, part):
-        planes = pl.ds(*y_parts[part])
-        remote(
-            held(sweep).at[planes, 0], yland.at[sweep - 1, planes], y_send.at[sweep - 1, part],
-            y_recv.at[sweep - 1, part], partner,
-        ).wait_send()
-
-    for sweep in range(1, SWEEPS + 1):
-        for side in range(2 if sweep < SWEEPS else 1):
-            for part in range(2):
-                left_z(sweep, side, part)
-
-        def all_y():
-            for part in range(4):
-                left_y(sweep, part)
-        only_if_last(sweep, all_y)
-
-
-def relax_and_gram(snap, classes, yface, zface, face, members):
-    own, rows_all, depth, width = snap.shape
-    both, rows = 2 * own, rows_all // 2
-    vmem = pl.BlockSpec(memory_space=pltpu.VMEM)
-    f32, bf16 = jnp.float32, jnp.bfloat16
-    dma = pltpu.SemaphoreType.DMA
-    return pl.pallas_call(
-        functools.partial(relax_kernel, members=members),
-        out_shape=(
-            jax.ShapeDtypeStruct((both, rows, depth, width), bf16),
-            jax.ShapeDtypeStruct((2 * width, width), f32),
-        ),
-        in_specs=[vmem] * 5,
-        out_specs=(vmem, vmem),
-        scratch_shapes=[
-            pltpu.VMEM((2, both + 2, rows + 2, depth + 16, width), f32),
-            pltpu.VMEM((8, both, rows, depth, width), f32),
-            pltpu.VMEM((8, both, rows_all, depth), f32),
-            pltpu.VMEM((4 * rows, rows * width), bf16),
-            pltpu.VMEM((both + 2, rows_all, depth), f32),
-            pltpu.VMEM((2, rows_all, width), f32),
-            pltpu.VMEM((SWEEPS - 1, both, rows, depth, width), bf16),
-            pltpu.VMEM((own, rows + 1, depth, width), bf16),
-            pltpu.VMEM((SWEEPS + 1, 2, rows, depth, width), bf16),
-            pltpu.VMEM((SWEEPS, both, depth, width), bf16),
-            pltpu.VMEM((max(both, rows), depth, 3 * width), bf16),
-            pltpu.VMEM((own, rows_all, depth), jnp.int32),
-            pltpu.VMEM((rows_all, depth), jnp.int32),
-            pltpu.VMEM((rows_all, depth), jnp.int32),
-            dma((own,)),
-            dma((own,)),
-            dma((SWEEPS + 1, 2, 2)),
-            dma((SWEEPS + 1, 2, 2)),
-            dma((SWEEPS, 4)),
-            dma((SWEEPS, 4)),
-            dma((3,)),
-            dma((3,)),
-        ],
-        compiler_params=pltpu.CompilerParams(
-            collective_id=0, has_side_effects=True, vmem_limit_bytes=60 << 20
-        ),
-    )(snap, classes, yface, zface, face)
+    add_stiff(state_ref[both - 1], rows)
+
+    def drain():
+        class_copies[0].wait_send()
+        for place in range(2):
+            remote(
+                class_ref.at[0], class_low, class_send.at[1 + place], class_recv.at[1], partner
+            ).wait_send()
+        for copy in swaps:
+            copy.wait_send()
+        for side in range(2):
+            remote(
+                snap_ref.at[0, pl.ds(0, rows)], zland.at[0, 0], z_send.at[0, side, 0], z_recv.at[0, 0, 0], lower
+            ).wait_send()
+
+        def left_z(sweep, side, part):
+            cells = pl.ds(0, chunk)
+            remote(
+                held(sweep).at[0, cells], zland.at[sweep, 0, cells], z_send.at[sweep, side, part],
+                z_recv.at[sweep, 0, part], lower,
+            ).wait_send()
+
+        def left_y(sweep, part):
+            planes = pl.ds(*y_parts[part])
+            remote(
+                held(sweep).at[planes, 0], yland.at[sweep - 1, planes], y_send.at[sweep - 1, part],
+                y_recv.at[sweep - 1, part], partner,
+            ).wait_send()
+
+        for sweep in range(1, SWEEPS + 1):
+            for side in range(2 if sweep < SWEEPS else 1):
+                for part in range(2):
+                    left_z(sweep, side, part)
+
+            def all_y():
+                for part in range(4):
+                    left_y(sweep, part)
+            only_if_last(sweep, all_y)
+
+    return drain
 
 
 TILE = 8
@@ -597,34 +565,37 @@
     return jnp.concatenate([tile / jnp.sqrt(scale) for tile, scale in zip(right, scales)], axis=0)
 
 
-def modes_kernel(
-    snaps_ref, gram_ref, start_ref, corr_ref, out_ref,
-    slots, summed, total, stage, send_sem, recv_sem, send_two, recv_two, send_out, recv_out,
+def whole_kernel(
+    snap_ref, class_ref, yface_ref, zface_ref, face_ref, start_ref, corr_ref, out_ref,
+    field, coef, compact, select, kappa, ghost_z, early, swap, zland, yland, rhs,
+    class_pair, class_low, class_high, slab, slab_sem,
+    swap_send, swap_recv, z_send, z_recv, y_send, y_recv, class_send, class_recv,
+    state, mass_part, stiff_part, slots, summed, mass_total, stiff_total, stage,
+    sum_sem, send_out, recv_out,
     *, members, owners, own, cell_count,
 ):
     me_sub = lax.axis_index("sub")
     me_nbhd = lax.axis_index("nbhd")
-    size = gram_ref.shape[1]
-    chunk = 2 * size // members
-
-    def sub_at(step):
-        return lax.rem(me_sub + step, members)
-
+    size = mass_part.shape[1]
+    chunk = size // members
     half = lax.rem(me_sub, 2)
     tower = me_sub - half
-    planes = own
-    across = owners // planes
+    across = owners // own
     mine = across // 2
     from_half = lax.rem(me_nbhd, across) // mine
     whole = jnp.where(from_half == half, 1, 0)
 
+    pltpu.make_async_copy(snap_ref, slab, slab_sem).start()
+
+    def sub_at(step):
+        return lax.rem(me_sub + step, members)
+
+    def is_me(nbhd):
+        return jnp.logical_and(nbhd == me_nbhd, from_half == half)
+
     barrier = pltpu.get_barrier_semaphore()
     for step in range(1, members):
         pl.semaphore_signal(barrier, inc=1, device_id=(me_nbhd, sub_at(step)), device_id_type=MESH)
-
-    def is_me(nbhd):
-        return jnp.logical_and(nbhd == me_nbhd, from_half == half)
-
     for nbhd in range(owners):
         @pl.when(jnp.logical_not(is_me(nbhd)))
         def _():
@@ -633,50 +604,69 @@
             )
     pl.semaphore_wait(barrier, members - 1 + owners - whole)
 
-    def part(owner):
-        return pl.ds(pl.multiple_of(owner * chunk, chunk), chunk)
-
-    copies = []
-    for step in range(1, members):
-        peer = sub_at(step)
-        copy = pltpu.make_async_remote_copy(
-            src_ref=gram_ref.at[part(peer)],
-            dst_ref=slots.at[step],
-            send_sem=send_sem.at[step],
-            recv_sem=recv_sem.at[step],
-            device_id=(me_nbhd, peer),
-            device_id_type=MESH,
-        )
-        copy.start()
-        copies.append(copy)
-    acc = gram_ref[part(me_sub)]
-    for step in range(1, members):
-        copies[step - 1].wait_recv()
-        acc = acc + slots[step]
-    summed[...] = acc
-    total[part(me_sub)] = acc
-    spread = []
-    for step in range(1, members):
-        copy = pltpu.make_async_remote_copy(
-            src_ref=summed,
-            dst_ref=total.at[part(me_sub)],
-            send_sem=send_two.at[step],
-            recv_sem=recv_two.at[step],
-            device_id=(me_nbhd, sub_at(step)),
-            device_id_type=MESH,
-        )
-        copy.start()
-        spread.append(copy)
-    for copy in spread:
-        copy.wait_recv()
+    def rows_of(sub):
+        return pl.ds(pl.multiple_of(sub * chunk, chunk), chunk)
+
+    def scatter(which, partial_ref):
+        copies = []
+        for step in range(1, members):
+            peer = sub_at(step)
+            copy = pltpu.make_async_remote_copy(
+                src_ref=partial_ref.at[rows_of(peer)],
+                dst_ref=slots.at[which, step],
+                send_sem=sum_sem.at[which, 0, step],
+                recv_sem=sum_sem.at[which, 1, step],
+                device_id=(me_nbhd, peer),
+                device_id_type=MESH,
+            )
+            copy.start()
+            copies.append(copy)
+        return copies
+
+    def share(which, partial_ref, total_ref, copies):
+        acc = partial_ref[rows_of(me_sub)]
+        for step in range(1, members):
+            copies[step - 1].wait_recv()
+            acc = acc + slots[which, step]
+        summed[which] = acc
+        total_ref[rows_of(me_sub)] = acc
+        spreads = []
+        for step in range(1, members):
+            copy = pltpu.make_async_remote_copy(
+                src_ref=summed.at[which],
+                dst_ref=total_ref.at[rows_of(me_sub)],
+                send_sem=sum_sem.at[which, 2, step],
+                recv_sem=sum_sem.at[which, 3, step],
+                device_id=(me_nbhd, sub_at(step)),
+                device_id_type=MESH,
+            )
+            copy.start()
+            spreads.append(copy)
+        return spreads
+
+    sent = []
+    drain = relax_part(
+        snap_ref, class_ref, yface_ref, zface_ref, face_ref, state, mass_part, stiff_part,
+        field, coef, compact, select, kappa, ghost_z, early, swap, zland, yland, rhs,
+        class_pair, class_low, class_high, slab, slab_sem,
+        swap_send, swap_recv, z_send, z_recv, y_send, y_recv, class_send, class_recv,
+        members, lambda: sent.append(scatter(0, mass_part)),
+    )
+    sent.append(scatter(1, stiff_part))
+    sent.append(share(0, mass_part, mass_total, sent[0]))
+    sent.append(share(1, stiff_part, stiff_total, sent[1]))
 
     dot = functools.partial(
         lax.dot_general, precision=lax.Precision.HIGHEST, preferred_element_type=jnp.float32
     )
-    mass = total[:size] / cell_count
-    stiff = total[size:]
+    for copy in sent[3]:
+        copy.wait_recv()
+    stiff = stiff_total[...]
     stiff = (stiff + stiff.T) * (0.5 / cell_count)
     inverse = eliminate_spd(stiff, size, 32)
+    for copy in sent[2]:
+        copy.wait_recv()
+    mass = mass_total[...] / cell_count
     step_map = dot(mass, inverse, (((1,), (0,)), ((), ())))
     both = jnp.concatenate([step_map, dot(step_map, mass, (((1,), (0,)), ((), ())))], axis=1)
     rows = start_ref[...]
@@ -688,9 +678,13 @@
         rows = normalize(inner, solved)
     modes = rows.astype(jnp.bfloat16)
 
+    lines = state.shape[1] // mine
+
     def piece(index, owner):
         values = lax.dot_general(
-            modes, snaps_ref[index], (((1,), (1,)), ((), ())), preferred_element_type=jnp.float32
+            modes, state[index // mine, pl.ds(lax.rem(index, mine) * lines, lines)].reshape(
+                lines * state.shape[2], size
+            ), (((1,), (1,)), ((), ())), preferred_element_type=jnp.float32,
         )
         return (values * corr_ref[me_nbhd, owner].astype(jnp.float32)).astype(jnp.bfloat16)
 
@@ -708,8 +702,8 @@
     for step in range(owners):
         index = lax.rem(step + me_nbhd, owners)
         level = index // mine
-        owner = across * lax.rem(level, planes) + mine * half + lax.rem(index, mine)
-        sub = tower + level // planes
+        owner = across * lax.rem(level, own) + mine * half + lax.rem(index, mine)
+        sub = tower + level // own
         here = jnp.logical_and(owner == me_nbhd, sub == me_sub)
         stage[step] = piece(index, owner)
 
@@ -733,49 +727,73 @@
         @pl.when(jnp.logical_not(here))
         def _():
             leave(step, owner, sub).wait_send()
-    for copy in copies + spread:
-        copy.wait_send()
-
-
-def modes_and_pieces(snaps, gram, start, corr, members, owners, own, cell_count):
-    pieces, cells, size = snaps.shape
-    modes = start.shape[0]
+    for copies in sent:
+        for copy in copies:
+            copy.wait_send()
+    drain()
+
+
+def on_device(snap_init, channel_map, yface_vals, zface_vals, face_of, start_block, correlation):
+    own, rows_all, depth, width = snap_init.shape[1:]
+    modes = start_block.shape[2]
+    members, owners = lax.axis_size("sub"), lax.axis_size("nbhd")
+    both, rows = 2 * own, rows_all // 2
+    cells = own * rows_all * depth
+    chunk = width // members
     vmem = pl.BlockSpec(memory_space=pltpu.VMEM)
-    return pl.pallas_call(
+    f32, bf16 = jnp.float32, jnp.bfloat16
+    dma = pltpu.SemaphoreType.DMA
+    result = pl.pallas_call(
         functools.partial(
-            modes_kernel, members=members, owners=owners, own=own, cell_count=cell_count
+            whole_kernel, members=members, owners=owners, own=own, cell_count=float(cells * members)
         ),
-        out_shape=jax.ShapeDtypeStruct((owners, modes, cells), jnp.bfloat16),
-        in_specs=[vmem, vmem, vmem, pl.BlockSpec(memory_space=pltpu.SMEM)],
+        out_shape=jax.ShapeDtypeStruct((owners, modes, cells // owners), bf16),
+        in_specs=[pl.BlockSpec(memory_space=pl.ANY)] + [vmem] * 5
+        + [pl.BlockSpec(memory_space=pltpu.SMEM)],
         out_specs=vmem,
         scratch_shapes=[
-            pltpu.VMEM((members, 2 * size // members, size), jnp.float32),
-            pltpu.VMEM((2 * size // members, size), jnp.float32),
-            pltpu.VMEM((2 * size, size), jnp.float32),
-            pltpu.VMEM((owners, modes, cells), jnp.bfloat16),
-            pltpu.SemaphoreType.DMA((members,)),
-            pltpu.SemaphoreType.DMA((members,)),
-            pltpu.SemaphoreType.DMA((members,)),
-            pltpu.SemaphoreType.DMA((members,)),
-            pltpu.SemaphoreType.DMA((owners,)),
-            pltpu.SemaphoreType.DMA((owners,)),
+            pltpu.VMEM((2, both + 2, rows + 2, depth + 16, width), f32),
+            pltpu.VMEM((8, both, rows, depth, width), f32),
+            pltpu.VMEM((8, both, rows_all, depth), f32),
+            pltpu.VMEM((4 * rows, rows * width), bf16),
+            pltpu.VMEM((both + 2, rows_all, depth), f32),
+            pltpu.VMEM((2, rows_all, width), f32),
+            pltpu.VMEM((SWEEPS - 1, both, rows, depth, width), bf16),
+            pltpu.VMEM((own, rows + 1, depth, width), bf16),
+            pltpu.VMEM((SWEEPS + 1, 2, rows, depth, width), bf16),
+            pltpu.VMEM((SWEEPS, both, depth, width), bf16),
+            pltpu.VMEM((max(both, rows), depth, 2 * width), bf16),
+            pltpu.VMEM((own, rows_all, depth), jnp.int32),
+            pltpu.VMEM((rows_all, depth), jnp.int32),
+            pltpu.VMEM((rows_all, depth), jnp.int32),
+            pltpu.VMEM((own, rows_all, depth, width), bf16),
+            dma,
+            dma((own,)),
+            dma((own,)),
+            dma((SWEEPS + 1, 2, 2)),
+            dma((SWEEPS + 1, 2, 2)),
+            dma((SWEEPS, 4)),
+            dma((SWEEPS, 4)),
+            dma((3,)),
+            dma((3,)),
+            pltpu.VMEM((both, rows, depth, width), bf16),
+            pltpu.VMEM((width, width), f32),
+            pltpu.VMEM((width, width), f32),
+            pltpu.VMEM((2, members, chunk, width), f32),
+            pltpu.VMEM((2, chunk, width), f32),
+            pltpu.VMEM((width, width), f32),
+            pltpu.VMEM((width, width), f32),
+            pltpu.VMEM((owners, modes, cells // owners), bf16),
+            dma((2, 4, members)),
+            dma((owners,)),
+            dma((owners,)),
         ],
         compiler_params=pltpu.CompilerParams(
-            collective_id=1, has_side_effects=True, vmem_limit_bytes=32 << 20
+            collective_id=0, has_side_effects=True, vmem_limit_bytes=60 << 20
         ),
-    )(snaps, gram, start, corr)
-
-
-def on_device(snap_init, channel_map, yface_vals, zface_vals, face_of, start_block, correlation):
-    own, rows, depth, width = snap_init.shape[1:]
-    members, owners = lax.axis_size("sub"), lax.axis_size("nbhd")
-    state, gram = relax_and_gram(
-        snap_init[0], channel_map[0], yface_vals[0], zface_vals[0], face_of, members
-    )
-    cells = own * rows * depth
-    result = modes_and_pieces(
-        state.reshape(owners, cells // owners, width), gram, start_block[0].T, correlation,
-        members, owners, own, float(cells * members),
+    )(
+        snap_init[0], channel_map[0], yface_vals[0], zface_vals[0], face_of, start_block[0].T,
+        correlation,
     )
     return result[None, None]
 

time: 93.4 us -> 87.7 us (0.939)
  Pallas kernels: 89.4 us -> 85.7 us
  local copies, waits for them, and re-layouts: 3.06 us -> 1.78 us
    pallas_call x2 -> x1, Pallas kernels: 89.4 us -> 85.7 us  [on_device(): pl.pallas_call(functools.partial(whole_kernel, members=members, owners=ow...]
    unnamed x9 -> x1, local copies, waits for them, and re-layouts: 3.06 us -> 1.78 us
where the time goes in v6:
time: 87.7 us; the launch traced here: 87.5 us
  Pallas kernels  85.7 us (98%)
  local copies, waits for them, and re-layouts  1.78 us (2%)
    pallas_call x1, Pallas kernels, on_device(): pl.pallas_call(functools.partial(whole_kernel, members=members, owners=ow...  85.7 us
    unnamed x1, local copies, waits for them, and re-layouts  1.78 us

profile of v6, /device:TPU:1, one launch (start us, length us, event | category | flops | bytes accessed | tf_op | source)
XLA Modules:
  0.0 87.5 jit_solution(9268784485571608424)
XLA Ops:
  0.0 85.7 %shard_map.73 = bf16[16,32,384]{2,1,0:T(8,128)(2,1)} custom-call(bf16[4,16,96,128]{3,2,1,0:T(8,128)(2,1)} %bitcast.8, s32[4,16,96]{2,1,0:T(8,128)} %bitcast.10, bf16[96,128]{1,0:T(8,128)(2,1)} %bitcast.11, bf16[16,128]{1,0:T(8,128)(2,1)} %bitcast.13, s32[1,128]{1,0:T(1,128)} %face_ref.1, f32[32,128]{1,0:T(8,128)} %bitcast.12, s32[16,16]{1,0:T(8,128)} %corr_ref.1), custom_call_target="tpu_custom_call" | custom-call | tf_op jit(solution)/shard_map/pallas_call | solution.py:746
  85.7 1.8 %copy.9 = bf16[1,1,16,32,384]{4,3,2,1,0:T(8,128)(2,1)} copy(bf16[1,1,16,32,384]{4,3,2,1,0:T(8,128)(2,1)} %bitcast.9) | data formatting | bytes 786432

commit v7 on v6

--- a/solution.py
+++ b/solution.py
@@ -319,6 +319,7 @@
                 send_z(1, side, 0)
                 send_z(1, side, 1)
                 send_y(1, 2 + side, side * (both - 1), 1)
+            widen((6, 7))
         if turn >= 2:
             line(1, plane_of(q + 2), 1, rows)
         if q == own - 1:
@@ -341,25 +342,24 @@
             line(sweep, i + 2, 1 + half, rows - 1)
             return 0
         lax.fori_loop(0, both - 2, middle, 0)
-        if sweep >= SWEEPS - 1:
-            widen((8 - 1 - SWEEPS + sweep,))
+
+        def border(part):
+            take_y(src, sweep - 1, part)
+            first, count = y_parts[part]
+
+            def body(i, _):
+                row(sweep, first + i + 1, edge)
+                return 0
+            lax.fori_loop(0, count, body, 0)
+            only_if_last(sweep, lambda: send_y(sweep, part, first, count))
+
+        border(0)
         for side in (0, 1):
             take_z(src, sweep - 1, side, 0)
             line(sweep, 1 + side * (both - 1), 1 + chunk_at(0), chunk)
             if side in sides:
                 send_z(sweep, side, 0)
-        take_y(src, sweep - 1, 0)
-        take_y(src, sweep - 1, 1)
-
-        def border(i, _):
-            row(sweep, i + 2, edge)
-            return 0
-        lax.fori_loop(0, both - 2, border, 0)
-
-        def first_parts():
-            send_y(sweep, 0, *y_parts[0])
-            send_y(sweep, 1, *y_parts[1])
-        only_if_last(sweep, first_parts)
+        border(1)
         for side in (0, 1):
             take_y(src, sweep - 1, 2 + side)
             take_z(src, sweep - 1, side, 1)
@@ -789,7 +789,7 @@
             dma((owners,)),
         ],
         compiler_params=pltpu.CompilerParams(
-            collective_id=0, has_side_effects=True, vmem_limit_bytes=60 << 20
+            collective_id=0, has_side_effects=True, vmem_limit_bytes=52 << 20
         ),
     )(
         snap_init[0], channel_map[0], yface_vals[0], zface_vals[0], face_of, start_block[0].T,

time: 87.7 us -> 91.1 us (1.039)
  local copies, waits for them, and re-layouts: 1.78 us -> 5 us
    unnamed x1 -> x13, local copies, waits for them, and re-layouts: 1.78 us -> 5 us
where the time goes in v7:
time: 91.1 us; the launch traced here: 90.7 us
  Pallas kernels  85.7 us (94%)
  local copies, waits for them, and re-layouts  5 us (5%)
    pallas_call x1, Pallas kernels, on_device(): pl.pallas_call(functools.partial(whole_kernel, members=members, owners=ow...  85.7 us
    unnamed x13, local copies, waits for them, and re-layouts  5 us

profile of v7, /device:TPU:1, one launch (start us, length us, event | category | flops | bytes accessed | tf_op | source)
XLA Modules:
  0.0 90.7 jit_solution(3990953792122168665)
XLA Ops:
  0.0 0.0 copy-start
  0.0 0.8 copy-done
  0.8 0.0 copy-start.1
  0.8 0.7 copy-done.1
  1.5 0.0 copy-start.2
  1.5 0.7 copy-done.2
  2.2 0.0 copy-start.3
  2.2 0.7 copy-done.3
  2.9 0.0 copy-start.4
  2.9 0.7 copy-done.4
  3.6 0.0 copy-start.5
  3.6 0.7 copy-done.5
  4.3 85.7 %shard_map.73 = bf16[16,32,384]{2,1,0:T(8,128)(2,1)S(1)} custom-call(bf16[4,16,96,128]{3,2,1,0:T(8,128)(2,1)} %bitcast.13, s32[4,16,96]{2,1,0:T(8,128)S(1)} %bitcast.9, bf16[96,128]{1,0:T(8,128)(2,1)S(1)} %bitcast.10, bf16[16,128]{1,0:T(8,128)(2,1)S(1)} %bitcast.12, s32[1,128]{1,0:T(1,128)S(1)} %copy-done.5, f32[32,128]{1,0:T(8,128)S(1)} %bitcast.11, ...), custom_call_target="tpu_custom_call" | custom-call | tf_op jit(solution)/shard_map/pallas_call | solution.py:746
  90.0 0.7 copy.9
Async XLA Ops:
  0.0 0.8 copy-start
  0.8 0.7 copy-start.1
  1.5 0.7 copy-start.2
  2.2 0.7 copy-start.3
  2.9 0.7 copy-start.4
  3.6 0.7 copy-start.5

commit v8 on v6

--- a/solution.py
+++ b/solution.py
@@ -22,7 +22,7 @@
     field, coef, compact, select, kappa, ghost_z, early, swap, zland, yland, rhs,
     class_pair, class_low, class_high, slab, slab_sem,
     swap_send, swap_recv, z_send, z_recv, y_send, y_recv, class_send, class_recv,
-    members, mass_ready,
+    members, stiff_ready,
 ):
     me_nbhd = lax.axis_index("nbhd")
     me = lax.axis_index("sub")
@@ -202,7 +202,24 @@
             return 0
         lax.fori_loop(0, both, one, 0)
 
-    widen(range(6))
+    widen(range(3))
+    swaps[0].wait_recv()
+
+    @pl.when(half == 0)
+    def _():
+        remote(
+            swap.at[0, pl.ds(0, rows)], zland.at[0, 0], z_send.at[0, 1, 0], z_recv.at[0, 0, 0],
+            upper,
+        ).start()
+
+    @pl.when(half == 1)
+    def _():
+        remote(
+            swap.at[0, pl.ds(1, rows)], zland.at[0, 1], z_send.at[0, 0, 0], z_recv.at[0, 1, 0],
+            lower,
+        ).start()
+
+    widen(range(3, 6))
 
     def row(sweep, p, y):
         src, dst = (sweep + 1) % 2, sweep % 2
@@ -284,26 +301,13 @@
     def plane_of(e):
         return e + (1 - half) * (top - 2 * e)
 
-    for e in range(own + 2, both):
+    ahead = range(own + 2, both)
+    for e in ahead:
         line(1, plane_of(e), 1, rows)
     for turn, q in enumerate(order):
-        swaps[turn].wait_recv()
+        if turn:
+            swaps[turn].wait_recv()
         plane = q + (1 - half) * (own - 1 - 2 * q)
-        if turn == 0:
-            @pl.when(half == 0)
-            def _():
-                remote(
-                    swap.at[0, pl.ds(0, rows)], zland.at[0, 0], z_send.at[0, 1, 0], z_recv.at[0, 0, 0],
-                    upper,
-                ).start()
-
-            @pl.when(half == 1)
-            def _():
-                remote(
-                    swap.at[0, pl.ds(1, rows)], zland.at[0, 1], z_send.at[0, 0, 0], z_recv.at[0, 1, 0],
-                    lower,
-                ).start()
-
         def fill(r, _):
             field[0, 1 + own * (1 - half) + plane, shift + r, inner, :] = swap[turn, r].astype(
                 jnp.float32
@@ -323,6 +327,9 @@
             line(1, plane_of(q + 2), 1, rows)
         if q == own - 1:
             send_y(1, half, 1 + (own - 1) * half, own - 1)
+            widen((6, 7))
+            for e in ahead:
+                line(2, plane_of(e), 1 + half, rows - 1)
     line(1, plane_of(3), 1, rows)
     line(1, plane_of(2), 1, rows)
     send_y(1, 1 - half, 1 + (own - 1) * (1 - half), own - 1)
@@ -338,11 +345,9 @@
         sides = (0, 1) if sweep < SWEEPS else (0,)
 
         def middle(i, _):
-            line(sweep, i + 2, 1 + half, rows - 1)
-            return 0
-        lax.fori_loop(0, both - 2, middle, 0)
-        if sweep >= SWEEPS - 1:
-            widen((8 - 1 - SWEEPS + sweep,))
+            line(sweep, plane_of(i + 2), 1 + half, rows - 1)
+            return 0
+        lax.fori_loop(0, both - 2 - (len(ahead) if sweep == 2 else 0), middle, 0)
         for side in (0, 1):
             take_z(src, sweep - 1, side, 0)
             line(sweep, 1 + side * (both - 1), 1 + chunk_at(0), chunk)
@@ -406,9 +411,6 @@
         lax.fori_loop(0, rows, body, 0)
         mass_ref[...] += gram(state_ref[p], rows, width)
         return 0
-    lax.fori_loop(0, both, weigh, 0)
-    mass_ready()
-
     def inside(i, _):
         def body(y, _):
             stiff_row(i + 1, y + 1, y)
@@ -417,6 +419,7 @@
         add_stiff(state_ref[i, pl.ds(0, rows - 1)], rows - 1)
         return 0
     lax.fori_loop(0, both - 1, inside, 0)
+    lax.fori_loop(0, own - 1, weigh, 0)
 
     @pl.when(half == 0)
     def _():
@@ -443,6 +446,8 @@
         return 0
     lax.fori_loop(0, rows, roof, 0)
     add_stiff(state_ref[both - 1], rows)
+    stiff_ready()
+    lax.fori_loop(own - 1, both, weigh, 0)
 
     def drain():
         class_copies[0].wait_send()
@@ -650,21 +655,21 @@
         field, coef, compact, select, kappa, ghost_z, early, swap, zland, yland, rhs,
         class_pair, class_low, class_high, slab, slab_sem,
         swap_send, swap_recv, z_send, z_recv, y_send, y_recv, class_send, class_recv,
-        members, lambda: sent.append(scatter(0, mass_part)),
+        members, lambda: sent.append(scatter(1, stiff_part)),
     )
-    sent.append(scatter(1, stiff_part))
-    sent.append(share(0, mass_part, mass_total, sent[0]))
-    sent.append(share(1, stiff_part, stiff_total, sent[1]))
+    sent.append(scatter(0, mass_part))
+    sent.append(share(1, stiff_part, stiff_total, sent[0]))
+    sent.append(share(0, mass_part, mass_total, sent[1]))
 
     dot = functools.partial(
         lax.dot_general, precision=lax.Precision.HIGHEST, preferred_element_type=jnp.float32
     )
-    for copy in sent[3]:
+    for copy in sent[2]:
         copy.wait_recv()
     stiff = stiff_total[...]
     stiff = (stiff + stiff.T) * (0.5 / cell_count)
     inverse = eliminate_spd(stiff, size, 32)
-    for copy in sent[2]:
+    for copy in sent[3]:
         copy.wait_recv()
     mass = mass_total[...] / cell_count
     step_map = dot(mass, inverse, (((1,), (0,)), ((), ())))

time: 87.7 us -> 87.2 us (level)
  no operation moved by 1% of the time
where the time goes in v8:
time: 87.2 us; the launch traced here: 87 us
  Pallas kernels  85.2 us (98%)
  local copies, waits for them, and re-layouts  1.78 us (2%)
    pallas_call x1, Pallas kernels, on_device(): pl.pallas_call(functools.partial(whole_kernel, members=members, owners=ow...  85.2 us
    unnamed x1, local copies, waits for them, and re-layouts  1.78 us

profile of v8, /device:TPU:1, one launch (start us, length us, event | category | flops | bytes accessed | tf_op | source)
XLA Modules:
  0.0 87.0 jit_solution(5437017154109625897)
XLA Ops:
  0.0 85.2 %shard_map.73 = bf16[16,32,384]{2,1,0:T(8,128)(2,1)} custom-call(bf16[4,16,96,128]{3,2,1,0:T(8,128)(2,1)} %bitcast.8, s32[4,16,96]{2,1,0:T(8,128)} %bitcast.10, bf16[96,128]{1,0:T(8,128)(2,1)} %bitcast.11, bf16[16,128]{1,0:T(8,128)(2,1)} %bitcast.13, s32[1,128]{1,0:T(1,128)} %face_ref.1, f32[32,128]{1,0:T(8,128)} %bitcast.12, s32[16,16]{1,0:T(8,128)} %corr_ref.1), custom_call_target="tpu_custom_call" | custom-call | tf_op jit(solution)/shard_map/pallas_call | solution.py:751
  85.2 1.8 %copy.9 = bf16[1,1,16,32,384]{4,3,2,1,0:T(8,128)(2,1)} copy(bf16[1,1,16,32,384]{4,3,2,1,0:T(8,128)(2,1)} %bitcast.9) | data formatting | bytes 786432

commit v9 on v8

--- a/solution.py
+++ b/solution.py
@@ -348,23 +348,23 @@
             line(sweep, plane_of(i + 2), 1 + half, rows - 1)
             return 0
         lax.fori_loop(0, both - 2 - (len(ahead) if sweep == 2 else 0), middle, 0)
+        def border(part):
+            take_y(src, sweep - 1, part)
+            first, count = y_parts[part]
+
+            def body(i, _):
+                row(sweep, first + i + 1, edge)
+                return 0
+            lax.fori_loop(0, count, body, 0)
+            only_if_last(sweep, lambda: send_y(sweep, part, first, count))
+
         for side in (0, 1):
             take_z(src, sweep - 1, side, 0)
             line(sweep, 1 + side * (both - 1), 1 + chunk_at(0), chunk)
             if side in sides:
                 send_z(sweep, side, 0)
-        take_y(src, sweep - 1, 0)
-        take_y(src, sweep - 1, 1)
-
-        def border(i, _):
-            row(sweep, i + 2, edge)
-            return 0
-        lax.fori_loop(0, both - 2, border, 0)
-
-        def first_parts():
-            send_y(sweep, 0, *y_parts[0])
-            send_y(sweep, 1, *y_parts[1])
-        only_if_last(sweep, first_parts)
+        border(0)
+        border(1)
         for side in (0, 1):
             take_y(src, sweep - 1, 2 + side)
             take_z(src, sweep - 1, side, 1)

time: 87.2 us -> 85.8 us (0.984)
  Pallas kernels: 85.2 us -> 83.6 us
    pallas_call x1, Pallas kernels: 85.2 us -> 83.6 us  [on_device(): pl.pallas_call(functools.partial(whole_kernel, members=members, owners=ow...]
where the time goes in v9:
time: 85.8 us; the launch traced here: 85.3 us
  Pallas kernels  83.6 us (97%)
  local copies, waits for them, and re-layouts  1.78 us (2%)
    pallas_call x1, Pallas kernels, on_device(): pl.pallas_call(functools.partial(whole_kernel, members=members, owners=ow...  83.6 us
    unnamed x1, local copies, waits for them, and re-layouts  1.78 us

profile of v9, /device:TPU:1, one launch (start us, length us, event | category | flops | bytes accessed | tf_op | source)
XLA Modules:
  0.0 85.3 jit_solution(14739727891572624014)
XLA Ops:
  0.0 83.6 %shard_map.73 = bf16[16,32,384]{2,1,0:T(8,128)(2,1)} custom-call(bf16[4,16,96,128]{3,2,1,0:T(8,128)(2,1)} %bitcast.8, s32[4,16,96]{2,1,0:T(8,128)} %bitcast.10, bf16[96,128]{1,0:T(8,128)(2,1)} %bitcast.11, bf16[16,128]{1,0:T(8,128)(2,1)} %bitcast.13, s32[1,128]{1,0:T(1,128)} %face_ref.1, f32[32,128]{1,0:T(8,128)} %bitcast.12, s32[16,16]{1,0:T(8,128)} %corr_ref.1), custom_call_target="tpu_custom_call" | custom-call | tf_op jit(solution)/shard_map/pallas_call | solution.py:751
  83.6 1.8 %copy.9 = bf16[1,1,16,32,384]{4,3,2,1,0:T(8,128)(2,1)} copy(bf16[1,1,16,32,384]{4,3,2,1,0:T(8,128)(2,1)} %bitcast.9) | data formatting | bytes 786432

commit v10 on v9

--- a/solution.py
+++ b/solution.py
@@ -323,16 +323,18 @@
                 send_z(1, side, 0)
                 send_z(1, side, 1)
                 send_y(1, 2 + side, side * (both - 1), 1)
-        if turn >= 2:
+        if 2 <= turn < own - 1:
             line(1, plane_of(q + 2), 1, rows)
         if q == own - 1:
             send_y(1, half, 1 + (own - 1) * half, own - 1)
             widen((6, 7))
             for e in ahead:
                 line(2, plane_of(e), 1 + half, rows - 1)
-    line(1, plane_of(3), 1, rows)
-    line(1, plane_of(2), 1, rows)
+    for e in range(own, 1, -1):
+        row(1, plane_of(e), edge)
     send_y(1, 1 - half, 1 + (own - 1) * (1 - half), own - 1)
+    for e in range(own, 1, -1):
+        line(1, plane_of(e), 1 + half, rows - 1)
 
     def only_if_last(sweep, action):
         if sweep < SWEEPS:
@@ -599,7 +601,7 @@
         return jnp.logical_and(nbhd == me_nbhd, from_half == half)
 
     barrier = pltpu.get_barrier_semaphore()
-    for step in range(1, members):
+    for step in (1, 2, members - 2, members - 1):
         pl.semaphore_signal(barrier, inc=1, device_id=(me_nbhd, sub_at(step)), device_id_type=MESH)
     for nbhd in range(owners):
         @pl.when(jnp.logical_not(is_me(nbhd)))
@@ -607,7 +609,7 @@
             pl.semaphore_signal(
                 barrier, inc=1, device_id=(nbhd, tower + from_half), device_id_type=MESH
             )
-    pl.semaphore_wait(barrier, members - 1 + owners - whole)
+    pl.semaphore_wait(barrier, 4 + owners - whole)
 
     def rows_of(sub):
         return pl.ds(pl.multiple_of(sub * chunk, chunk), chunk)

time: 85.8 us -> 83.3 us (0.971)
  Pallas kernels: 83.6 us -> 81.3 us
    pallas_call x1, Pallas kernels: 83.6 us -> 81.3 us  [on_device(): pl.pallas_call(functools.partial(whole_kernel, members=members, owners=ow...]
where the time goes in v10:
time: 83.3 us; the launch traced here: 83.1 us
  Pallas kernels  81.3 us (98%)
  local copies, waits for them, and re-layouts  1.78 us (2%)
    pallas_call x1, Pallas kernels, on_device(): pl.pallas_call(functools.partial(whole_kernel, members=members, owners=ow...  81.3 us
    unnamed x1, local copies, waits for them, and re-layouts  1.78 us

profile of v10, /device:TPU:1, one launch (start us, length us, event | category | flops | bytes accessed | tf_op | source)
XLA Modules:
  0.0 83.1 jit_solution(14087942734947345607)
XLA Ops:
  0.0 81.3 %shard_map.73 = bf16[16,32,384]{2,1,0:T(8,128)(2,1)} custom-call(bf16[4,16,96,128]{3,2,1,0:T(8,128)(2,1)} %bitcast.8, s32[4,16,96]{2,1,0:T(8,128)} %bitcast.10, bf16[96,128]{1,0:T(8,128)(2,1)} %bitcast.11, bf16[16,128]{1,0:T(8,128)(2,1)} %bitcast.13, s32[1,128]{1,0:T(1,128)} %face_ref.1, f32[32,128]{1,0:T(8,128)} %bitcast.12, s32[16,16]{1,0:T(8,128)} %corr_ref.1), custom_call_target="tpu_custom_call" | custom-call | tf_op jit(solution)/shard_map/pallas_call | solution.py:753
  81.3 1.8 %copy.9 = bf16[1,1,16,32,384]{4,3,2,1,0:T(8,128)(2,1)} copy(bf16[1,1,16,32,384]{4,3,2,1,0:T(8,128)(2,1)} %bitcast.9) | data formatting | bytes 786432

commit v11 on v10

--- a/solution.py
+++ b/solution.py
@@ -421,7 +421,7 @@
         add_stiff(state_ref[i, pl.ds(0, rows - 1)], rows - 1)
         return 0
     lax.fori_loop(0, both - 1, inside, 0)
-    lax.fori_loop(0, own - 1, weigh, 0)
+    lax.fori_loop(0, own // 2, weigh, 0)
 
     @pl.when(half == 0)
     def _():
@@ -449,7 +449,7 @@
     lax.fori_loop(0, rows, roof, 0)
     add_stiff(state_ref[both - 1], rows)
     stiff_ready()
-    lax.fori_loop(own - 1, both, weigh, 0)
+    lax.fori_loop(own // 2, both, weigh, 0)
 
     def drain():
         class_copies[0].wait_send()

time: 83.3 us -> 83.5 us (level)
  no operation moved by 1% of the time
where the time goes in v11:
time: 83.5 us; the launch traced here: 83.3 us
  Pallas kernels  81.5 us (98%)
  local copies, waits for them, and re-layouts  1.78 us (2%)
    pallas_call x1, Pallas kernels, on_device(): pl.pallas_call(functools.partial(whole_kernel, members=members, owners=ow...  81.5 us
    unnamed x1, local copies, waits for them, and re-layouts  1.78 us

profile of v11, /device:TPU:1, one launch (start us, length us, event | category | flops | bytes accessed | tf_op | source)
XLA Modules:
  0.0 83.3 jit_solution(3376878116287260733)
XLA Ops:
  0.0 81.5 %shard_map.73 = bf16[16,32,384]{2,1,0:T(8,128)(2,1)} custom-call(bf16[4,16,96,128]{3,2,1,0:T(8,128)(2,1)} %bitcast.8, s32[4,16,96]{2,1,0:T(8,128)} %bitcast.10, bf16[96,128]{1,0:T(8,128)(2,1)} %bitcast.11, bf16[16,128]{1,0:T(8,128)(2,1)} %bitcast.13, s32[1,128]{1,0:T(1,128)} %face_ref.1, f32[32,128]{1,0:T(8,128)} %bitcast.12, s32[16,16]{1,0:T(8,128)} %corr_ref.1), custom_call_target="tpu_custom_call" | custom-call | tf_op jit(solution)/shard_map/pallas_call | solution.py:753
  81.5 1.8 %copy.9 = bf16[1,1,16,32,384]{4,3,2,1,0:T(8,128)(2,1)} copy(bf16[1,1,16,32,384]{4,3,2,1,0:T(8,128)(2,1)} %bitcast.9) | data formatting | bytes 786432
